TPU v7x, 32 devices: a whole 2x2x4 slice. The times are simulated.
32 devices in a mesh: groups: 2 (over x), col: 16 (over z, y, core).
Axes of the slice: x: 2, y: 2, z: 4, core: 2. Of those that a mesh axis runs over, the one named last changes fastest.
Arguments:
- trajectory: float32 [2048, 64], P('groups'), parts along dimension 0, may hold values from -6 to 6
- offsets: int32 [4], P('groups'), parts along dimension 0, may hold values from 0 to 896
- landmarks: float32 [16384, 64], replicated, may hold values from -6 to 6
- landmark_ids: int32 [16384], replicated, may hold values from 0 to 16383, each once
- inv_width: float32 [16384], replicated, may hold values from 0.25 to 2
- lower_pairs: float32 [6, 4096, 4096], P(None, 'col'), may hold values from -0.046875 to 0.046875
- diag_inverse: float32 [4, 4096, 4096], P(None, None, 'col')
Outputs:
- whitened: float32 [4, 4096, 512], P(None, 'col', 'groups'), parts along dimension 2
There are 2 independent parts, one for each index of `groups`. A program takes and returns all parts, laid end to end along the dimension named above; an argument that names none is the same for every part. Nothing has to cross between parts.
All inputs are finite; a program needn't handle non-finite values.
Results may differ from a plain program's by a relative error of at most 0.0001.
Values sent between devices are 32-bit elements; how exact they have to be, the bound alone decides.
No kernel may reach another device: no remote copies, remote signals or barrier semaphores. Data moves between devices by JAX's collectives and lax.ppermute only.
A program may use at most 128 MiB of HBM per device.

v0:
```python
import functools

import jax
import jax.numpy as jnp
from jax import lax
from jax.experimental import pallas as pl
from jax.experimental.pallas import tpu as pltpu
from jax.sharding import PartitionSpec as P


BATCH = 128
COL = "col"


def layout_of(mesh):
    axis = mesh.axis_names.index(COL)
    devices = mesh.devices
    line = devices.swapaxes(0, axis).reshape(devices.shape[axis], -1)[:, 0]
    count = len(line)
    cores = 1
    if count % 2 == 0 and getattr(line[0], "coords", 0) == getattr(line[1], "coords", 0):
        cores = 2
    chips = [line[i] for i in range(0, count, cores)]
    inner = 1
    if hasattr(chips[0], "coords") and len(chips) > 1:
        start = list(chips[0].coords)
        step = [a != b for a, b in zip(start, chips[1].coords)]
        inner = 1
        while inner < len(chips) and all(
            moved or a == b for moved, a, b in zip(step, start, chips[inner].coords)
        ):
            inner += 1
        if len(chips) % inner:
            inner = 1
    outer = len(chips) // inner
    if outer == 1:
        outer, inner = inner, 1
    return outer, inner, cores


class Grid:
    def __init__(self, extents):
        self.extents = extents
        self.count = extents[0] * extents[1] * extents[2]

    def split(self, index):
        _, inner, core = self.extents
        return index // (inner * core), (index // core) % inner, index % core

    def join(self, z, y, c):
        _, inner, core = self.extents
        return (z * inner + y) * core + c

    def shift(self, dz, dy, dc):
        pairs = []
        for index in range(self.count):
            z, y, c = self.split(index)
            pairs.append((index, self.join(*self.moved((z, y, c), (dz, dy, dc)))))
        return pairs

    def moved(self, place, by):
        out = []
        for at, step, size in zip(place, by, self.extents):
            power = size & (size - 1) == 0
            out.append(at ^ step if power else (at + step) % size)
        return tuple(out)

    def back(self, place, by):
        out = []
        for at, step, size in zip(place, by, self.extents):
            power = size & (size - 1) == 0
            out.append(at ^ step if power else (at - step) % size)
        return tuple(out)

    def send(self, value, dz=0, dy=0, dc=0):
        return lax.ppermute(value, COL, self.shift(dz, dy, dc))


def halves(value):
    high = value.astype(jnp.bfloat16)
    low = (value - high.astype(jnp.float32)).astype(jnp.bfloat16)
    return high, low


def three_pass(left, right):
    width = right.shape[1]
    left_high, left_low = halves(left)
    right_high, right_low = halves(right)
    both = jnp.concatenate([right_high, right_low], axis=1)
    main = jnp.dot(left_high, both, preferred_element_type=jnp.float32)
    rest = jnp.dot(left_low, right_high, preferred_element_type=jnp.float32)
    return main[:, :width] + (main[:, width:] + rest)


def lower_part(meta_ref, lower_ref, pair, pieces, owned, bufs):
    lbuf, wbuf, lsem, wsem, stage = bufs
    outer, _, zrows = lbuf.shape
    chunks, subs = len(pieces), len(pieces[0])
    width = wbuf.shape[2] // chunks
    from_z, from_sub = outer, 2 * outer + subs

    def l_copy(k):
        cols = pl.ds(pl.multiple_of(meta_ref[from_z + k] * zrows, zrows), zrows)
        return pltpu.make_async_copy(lower_ref.at[pair, :, cols], lbuf.at[k], lsem.at[k])

    def w_copy(m, sub, k):
        rows = pl.ds(pl.multiple_of(meta_ref[from_sub + sub] * owned, owned), owned)
        return pltpu.make_async_copy(
            pieces[m][sub].at[pl.ds(k * owned, owned), :],
            wbuf.at[k, rows, pl.ds(m * width, width)],
            wsem.at[(k * subs + sub) * chunks + m],
        )

    for k in range(outer):
        if stage != "lower":
            for sub in range(subs):
                for m in range(chunks):
                    w_copy(m, sub, k).start()
        l_copy(k).start()

    def finish(total):
        def step(k, carry):
            if stage != "lower":
                for sub in range(subs):
                    for m in range(chunks):
                        w_copy(m, sub, k).wait()
            l_copy(k).wait()
            return carry - three_pass(lbuf[k], wbuf[k])

        return lax.fori_loop(0, outer, step, total)

    return finish


def section_kernel(sec_idx, pair, subs, meta_ref, diag_ref, lower_ref, pending_ref, *refs):
    pieces = refs[:subs] if pair is not None else ()
    refs = refs[len(pieces) :]
    outs, refs = refs[:subs], refs[subs:]
    dbuf, obuf, xbuf, dsem, osem, xsem = refs[:6]
    outer, zrows, owned = dbuf.shape
    to_sub = 2 * outer
    x_copy = pltpu.make_async_copy(pending_ref, xbuf, xsem)
    x_copy.start()
    finish = None
    if pair is not None:
        lbuf, wbuf, lsem, wsem = refs[6:]
        finish = lower_part(meta_ref, lower_ref, pair, [pieces], owned, (lbuf, wbuf, lsem, wsem, "all"))

    def d_copy(k):
        rows = pl.ds(pl.multiple_of(meta_ref[k] * zrows, zrows), zrows)
        return pltpu.make_async_copy(diag_ref.at[sec_idx, rows, :], dbuf.at[k], dsem.at[k])

    def o_copy(sub, k):
        rows = pl.ds(pl.multiple_of(k * owned, owned), owned)
        return pltpu.make_async_copy(obuf.at[sub, rows, :], outs[sub].at[rows, :], osem.at[k * subs + sub])

    for k in range(outer):
        d_copy(k).start()
    x_copy.wait()
    x = xbuf[...]
    if finish is not None:
        x = finish(x)
    width = x.shape[1]
    x_high, x_low = halves(x)
    both = jnp.concatenate([x_high, x_low], axis=1)

    def step(k, carry):
        d_copy(k).wait()
        for sub in range(subs):
            rows = pl.ds(pl.multiple_of(meta_ref[to_sub + sub] * owned, owned), owned)
            high, low = halves(dbuf[k, rows, :])
            main = jnp.dot(high, both, preferred_element_type=jnp.float32)
            rest = jnp.dot(low, x_high, preferred_element_type=jnp.float32)
            at = pl.ds(pl.multiple_of(k * owned, owned), owned)
            obuf[sub, at, :] = main[:, :width] + (main[:, width:] + rest)
            o_copy(sub, k).start()
        return carry

    lax.fori_loop(0, outer, step, 0)
    for k in range(outer):
        for sub in range(subs):
            o_copy(sub, k).wait()


def section_product(grid, meta, diag_inverse, lower_pairs, pending, pieces, sec_idx, pair):
    outer, inner, cores = grid.extents
    subs = inner * cores
    owned, width = pending.shape
    zrows = subs * owned
    dma = pltpu.SemaphoreType.DMA
    scratch = [
        pltpu.VMEM((outer, zrows, owned), jnp.float32),
        pltpu.VMEM((subs, outer * owned, width), jnp.float32),
        pltpu.VMEM((owned, width), jnp.float32),
        dma((outer,)),
        dma((outer * subs,)),
        dma(()),
    ]
    if pair is not None:
        scratch += [
            pltpu.VMEM((outer, owned, zrows), jnp.float32),
            pltpu.VMEM((outer, zrows, width), jnp.float32),
            dma((outer,)),
            dma((outer * subs,)),
        ]
    anywhere = pl.BlockSpec(memory_space=pl.ANY)
    return pl.pallas_call(
        functools.partial(section_kernel, sec_idx, pair, subs),
        out_shape=[jax.ShapeDtypeStruct((outer * owned, width), jnp.float32)] * subs,
        in_specs=[pl.BlockSpec(memory_space=pltpu.SMEM)] + [anywhere] * (3 + len(pieces)),
        out_specs=[anywhere] * subs,
        scratch_shapes=scratch,
    )(meta, diag_inverse, lower_pairs, pending, *pieces)


def older_kernel(pairs, subs, chunks, meta_ref, lower_ref, *refs):
    count = len(pairs)
    pendings, refs = refs[: count * chunks], refs[count * chunks :]
    pieces = [refs[m * subs : (m + 1) * subs] for m in range(chunks)]
    refs = refs[chunks * subs :]
    outs, refs = refs[: count * chunks], refs[count * chunks :]
    wbuf, wsem = refs[:2]
    bufs, sems = refs[2 : 2 + count], refs[2 + count :]
    owned, width = outs[0].shape
    finishers = []
    for at, pair in enumerate(pairs):
        bound = (bufs[at], wbuf, sems[at], wsem, "all" if at == 0 else "lower")
        finishers.append(lower_part(meta_ref, lower_ref, pair, pieces, owned, bound))
    for at in range(count):
        mine = pendings[at * chunks : (at + 1) * chunks]
        total = finishers[at](jnp.concatenate([one[...] for one in mine], axis=1))
        for m in range(chunks):
            outs[at * chunks + m][...] = total[:, m * width : (m + 1) * width]


def older_product(grid, meta, lower_pairs, pendings, pieces, pairs):
    outer, inner, cores = grid.extents
    subs, chunks = inner * cores, len(pieces)
    owned, width = pendings[0][0].shape
    zrows = subs * owned
    dma = pltpu.SemaphoreType.DMA
    anywhere = pl.BlockSpec(memory_space=pl.ANY)
    vmem = pl.BlockSpec(memory_space=pltpu.VMEM)
    count = len(pairs)
    out = pl.pallas_call(
        functools.partial(older_kernel, pairs, subs, chunks),
        out_shape=[jax.ShapeDtypeStruct((owned, width), jnp.float32)] * (count * chunks),
        in_specs=[pl.BlockSpec(memory_space=pltpu.SMEM), anywhere]
        + [vmem] * (count * chunks)
        + [anywhere] * (subs * chunks),
        out_specs=[vmem] * (count * chunks),
        scratch_shapes=[pltpu.VMEM((outer, zrows, width * chunks), jnp.float32), dma((outer * subs * chunks,))]
        + [pltpu.VMEM((outer, owned, zrows), jnp.float32)] * count
        + [dma((outer,))] * count,
        name="older",
    )(meta, lower_pairs, *[one for row in pendings for one in row], *[one for row in pieces for one in row])
    return [out[at * chunks : (at + 1) * chunks] for at in range(count)]


def body(grid, trajectory, offsets, landmarks, landmark_ids, inv_width, lower_pairs, diag_inverse):
    nsec = diag_inverse.shape[0]
    sec = diag_inverse.shape[1]
    owned = diag_inverse.shape[2]
    features = landmarks.shape[1]
    outer, inner, cores = grid.extents
    me = lax.axis_index(COL)
    place = grid.split(me)
    first = me * owned

    def coordinates(step):
        zs = [step(place, (dz, 0, 0))[0] for dz in range(outer)]
        subs = []
        for dc in range(cores):
            for dy in range(inner):
                _, y, c = step(place, (0, dy, dc))
                subs.append(y * cores + c)
        return zs, subs

    to_z, to_sub = coordinates(grid.moved)
    from_z, from_sub = coordinates(grid.back)
    meta = jnp.stack(to_z + from_z + to_sub + from_sub).astype(jnp.int32)

    own_ids = lax.dynamic_slice_in_dim(landmark_ids.reshape(nsec, sec), first, owned, 1).reshape(-1)
    centers = jnp.take(landmarks, own_ids, axis=0)
    rates = jnp.take(inv_width, own_ids)
    center_sq = jnp.sum(centers * centers, axis=1)[:, None]
    chunks = offsets.shape[0]
    pending = []
    for m in range(chunks):
        snap = lax.dynamic_slice_in_dim(trajectory, offsets[m], BATCH, 0)
        cross = jnp.dot(centers, snap.T, precision=lax.Precision.HIGHEST, preferred_element_type=jnp.float32)
        dist = jnp.sum(snap * snap, axis=1)[None, :] + center_sq - 2.0 * cross
        kernel = jnp.exp(-rates[:, None] * dist / features)
        pending.append([kernel[s * owned : (s + 1) * owned] for s in range(nsec)])

    cut = lambda arr, i: arr[i * owned : (i + 1) * owned]

    def chunk_steps(m):
        pieces = ()
        for sec_idx in range(nsec):
            newest = sec_idx * (sec_idx - 1) // 2 + sec_idx - 1 if sec_idx else None
            yield
            parts = section_product(grid, meta, diag_inverse, lower_pairs, pending[m][sec_idx], pieces, sec_idx, newest)
            newest_pieces[m] = pieces
            own, rest = parts[:inner], parts[inner:]
            got = [
                [grid.send(rest[(dc - 1) * inner + dy], dc=dc) for dc in range(1, cores)]
                for dy in reversed(range(inner))
            ]
            yield
            plane = []
            for dy in range(1, inner):
                total = own[dy]
                for one in got[inner - 1 - dy]:
                    total = total + one
                plane.append(grid.send(total, dy=dy))
            yield
            mine = own[0]
            for one in got[-1] + plane:
                mine = mine + one
            got = [grid.send(cut(mine, dz), dz=dz) for dz in range(1, outer)]
            yield
            mine = cut(mine, 0)
            for one in got:
                mine = mine + one
            results[m][sec_idx] = mine
            if sec_idx + 1 == nsec:
                return
            got = [grid.send(mine, dz=dz) for dz in range(1, outer)]
            yield
            column = jnp.concatenate([mine] + got, axis=0)
            plane = [column] + [grid.send(column, dy=dy) for dy in range(1, inner)]
            across = [[grid.send(column, dc=dc)] for dc in range(1, cores)]
            yield
            for dc in range(1, cores):
                across[dc - 1] += [grid.send(one, dc=dc) for one in plane[1:]]
            pieces = tuple(plane + [one for row in across for one in row])

    def older_steps():
        for sec_idx in range(1, nsec - 1):
            later = range(sec_idx + 1, nsec)
            pairs = [s * (s - 1) // 2 + sec_idx - 1 for s in later]
            rows = [[pending[m][s] for m in range(chunks)] for s in later]
            done = older_product(grid, meta, lower_pairs, rows, newest_pieces, pairs)
            for s, row in zip(later, done):
                for m in range(chunks):
                    pending[m][s] = row[m]
            yield

    results = [[None] * nsec for _ in range(chunks)]
    newest_pieces = [None] * chunks
    steps = [chunk_steps(m) for m in range(chunks)] + [older_steps()]
    for one in steps[:chunks]:
        next(one)
    for who, _, _ in step_order(nsec, chunks):
        next(steps[who], None)
    return jnp.concatenate([jnp.stack(one, axis=0) for one in results], axis=2)


STEPS = 6


def step_order(nsec, chunks):
    keyed = []
    for sec_idx in range(nsec):
        for step in range(STEPS if sec_idx + 1 < nsec else STEPS - 2):
            at = sec_idx * STEPS + step
            lag = 0.5 if 0 < at < 5 else 1.5
            keyed += [(at + m * lag, at, (m, sec_idx, step)) for m in range(chunks)]
        if 0 < sec_idx < nsec - 1:
            at = sec_idx * STEPS + 1
            keyed.append((at + 1.5 * (chunks - 1), at + 1, (chunks, sec_idx, 0)))
    return [entry for _, _, entry in sorted(keyed)]


def solution(mesh):
    grid = Grid(layout_of(mesh))
    in_specs = (
        P("groups", None),
        P("groups"),
        P(),
        P(),
        P(),
        P(None, COL, None),
        P(None, None, COL),
    )
    out_specs = P(None, COL, "groups")
    step = jax.shard_map(
        functools.partial(body, grid), mesh=mesh, in_specs=in_specs, out_specs=out_specs, check_vma=False
    )

    def whole(trajectory, offsets, *rest):
        run = step
        return run(trajectory, offsets, *rest)

    return whole
```

profile of v0, /device:TPU:0, one launch (start us, length us, event | category | flops | bytes accessed | tf_op | source)
XLA Modules:
  0.0 392.3 jit_solution(10463966256634064790)
XLA Ops:
  4.0 7.0 %copy.9 = f32[16384,64]{1,0:T(8,128)} copy(f32[16384,64]{0,1:T(8,128)} %param.9) | data formatting | bytes 8388608 | tf_op args[2]
  11.1 6.2 %gather_fusion.1 = f32[1024,64]{1,0:T(8,128)S(1)} fusion(f32[16384,64]{1,0:T(8,128)} %copy.9, s32[1024]{0:T(1024)S(1)} %broadcast_clamp_fusion), kind=kCustom, calls=%fused_computation.1 | custom fusion | bytes 528384 | tf_op jit(solution)/shard_map/jit(_take)/gather | solution.py:284
  17.3 6.2 %gather_fusion = f32[1024]{0:T(1024)S(1)} fusion(f32[16384]{0:T(1024)S(1)} %copy-done, s32[1024]{0:T(1024)S(1)} %broadcast_clamp_fusion), kind=kCustom, calls=%fused_computation | custom fusion | bytes 12288 | tf_op jit(solution)/shard_map/jit(_take)/gather | solution.py:285
  45.9 10.1 %collective-permute-done.20 = f32[1024,128]{1,0:T(8,128)S(1)} collective-permute-done((f32[1024,128]{1,0:T(8,128)S(1)}, f32[1024,128]{1,0:T(8,128)S(1)}, u32[]{:S(2)}, u32[]{:S(2)}) %collective-permute-start.20) | collective-permute-done | bytes 524320 | tf_op jit(solution)/shard_map/ppermute | solution.py:76
  60.9 6.1 %collective-permute-done.2 = f32[1024,128]{1,0:T(8,128)S(1)} collective-permute-done((f32[1024,128]{1,0:T(8,128)S(1)}, f32[1024,128]{1,0:T(8,128)S(1)}, u32[]{:S(2)}, u32[]{:S(2)}) %collective-permute-start.2) | collective-permute-done | bytes 524320 | tf_op jit(solution)/shard_map/ppermute | solution.py:76
  81.0 7.9 %collective-permute-done.25 = f32[256,128]{1,0:T(8,128)S(1)} collective-permute-done((f32[256,128]{1,0:T(8,128)S(1)}, f32[256,128]{1,0:T(8,128)S(1)}, u32[]{:S(2)}, u32[]{:S(2)}) %collective-permute-start.25) | collective-permute-done | bytes 131104 | tf_op jit(solution)/shard_map/ppermute | solution.py:76
  109.2 11.7 %collective-permute-done.9.refs_1_.refs_5_ = f32[1024,128]{1,0:T(8,128)S(1)} collective-permute-done((f32[1024,128]{1,0:T(8,128)S(1)}, f32[1024,128]{1,0:T(8,128)S(1)}, u32[]{:S(2)}, u32[]{:S(2)}) %collective-permute-start.9) | collective-permute-done | bytes 524320 | tf_op jit(solution)/shard_map/ppermute | solution.py:76
  122.0 8.7 %shard_map.77 = (f32[1024,128]{1,0:T(8,128)}, f32[1024,128]{1,0:T(8,128)}, f32[1024,128]{1,0:T(8,128)}, f32[1024,128]{1,0:T(8,128)}) custom-call(s32[16]{0:T(128)} %stack.73.meta_ref, f32[4,4096,256]{2,1,0:T(8,128)} %diag_ref.15, f32[6,256,4096]{2,1,0:T(8,128)} %lower_ref.19, f32[256,128]{1,0:T(8,128)} %get-tuple-element.100.pending_ref, ...), custom_call_target="tpu_custom_call" | custom-call | tf_op jit(solution)/shard_map/pallas_call | solution.py:207
  131.3 8.9 %shard_map.74 = (f32[1024,128]{1,0:T(8,128)}, f32[1024,128]{1,0:T(8,128)}, f32[1024,128]{1,0:T(8,128)}, f32[1024,128]{1,0:T(8,128)}) custom-call(s32[16]{0:T(128)} %stack.73.meta_ref, f32[4,4096,256]{2,1,0:T(8,128)} %diag_ref.15, f32[6,256,4096]{2,1,0:T(8,128)} %lower_ref.19, f32[256,128]{1,0:T(8,128)} %get-tuple-element.107.pending_ref, ...), custom_call_target="tpu_custom_call" | custom-call | tf_op jit(solution)/shard_map/pallas_call | solution.py:207
  145.1 10.6 %collective-permute-done.44 = f32[1024,128]{1,0:T(8,128)S(1)} collective-permute-done((f32[1024,128]{1,0:T(8,128)S(1)}, f32[1024,128]{1,0:T(8,128)S(1)}, u32[]{:S(2)}, u32[]{:S(2)}) %collective-permute-start.44) | collective-permute-done | bytes 524320 | tf_op jit(solution)/shard_map/ppermute | solution.py:76
  176.7 7.8 %collective-permute-done.49 = f32[256,128]{1,0:T(8,128)S(1)} collective-permute-done((f32[256,128]{1,0:T(8,128)S(1)}, f32[256,128]{1,0:T(8,128)S(1)}, u32[]{:S(2)}, u32[]{:S(2)}) %collective-permute-start.49) | collective-permute-done | bytes 131104 | tf_op jit(solution)/shard_map/ppermute | solution.py:76
  206.6 11.7 %collective-permute-done.33.refs_1_.refs_3_ = f32[1024,128]{1,0:T(8,128)S(1)} collective-permute-done((f32[1024,128]{1,0:T(8,128)S(1)}, f32[1024,128]{1,0:T(8,128)S(1)}, u32[]{:S(2)}, u32[]{:S(2)}) %collective-permute-start.33) | collective-permute-done | bytes 524320 | tf_op jit(solution)/shard_map/ppermute | solution.py:76
  218.3 10.0 %older.2 = (f32[256,128]{1,0:T(8,128)}, f32[256,128]{1,0:T(8,128)}, f32[256,128]{1,0:T(8,128)}, f32[256,128]{1,0:T(8,128)}) custom-call(s32[16]{0:T(128)} %stack.73.meta_ref, f32[6,256,4096]{2,1,0:T(8,128)} %lower_ref.19, f32[256,128]{1,0:T(8,128)} %get-tuple-element.109.refs_0_, f32[256,128]{1,0:T(8,128)} %get-tuple-element.103.refs_1_, ...), custom_call_target="tpu_custom_call" | custom-call | tf_op jit(solution)/shard_map/older/pallas_call | solution.py:245
  229.4 8.7 %shard_map.79 = (f32[1024,128]{1,0:T(8,128)}, f32[1024,128]{1,0:T(8,128)}, f32[1024,128]{1,0:T(8,128)}, f32[1024,128]{1,0:T(8,128)}) custom-call(s32[16]{0:T(128)} %stack.73.meta_ref, f32[4,4096,256]{2,1,0:T(8,128)} %diag_ref.15, f32[6,256,4096]{2,1,0:T(8,128)} %lower_ref.19, f32[256,128]{1,0:T(8,128)} %get-tuple-element.71.pending_ref, ...), custom_call_target="tpu_custom_call" | custom-call | tf_op jit(solution)/shard_map/pallas_call | solution.py:207
  238.5 8.9 %shard_map.76 = (f32[1024,128]{1,0:T(8,128)}, f32[1024,128]{1,0:T(8,128)}, f32[1024,128]{1,0:T(8,128)}, f32[1024,128]{1,0:T(8,128)}) custom-call(s32[16]{0:T(128)} %stack.73.meta_ref, f32[4,4096,256]{2,1,0:T(8,128)} %diag_ref.15, f32[6,256,4096]{2,1,0:T(8,128)} %lower_ref.19, f32[256,128]{1,0:T(8,128)} %get-tuple-element.55.pending_ref, ...), custom_call_target="tpu_custom_call" | custom-call | tf_op jit(solution)/shard_map/pallas_call | solution.py:207
  252.3 10.6 %collective-permute-done.68 = f32[1024,128]{1,0:T(8,128)S(1)} collective-permute-done((f32[1024,128]{1,0:T(8,128)S(1)}, f32[1024,128]{1,0:T(8,128)S(1)}, u32[]{:S(2)}, u32[]{:S(2)}) %collective-permute-start.68) | collective-permute-done | bytes 524320 | tf_op jit(solution)/shard_map/ppermute | solution.py:76
  267.5 5.9 %collective-permute-done.38 = f32[1024,128]{1,0:T(8,128)S(1)} collective-permute-done((f32[1024,128]{1,0:T(8,128)S(1)}, f32[1024,128]{1,0:T(8,128)S(1)}, u32[]{:S(2)}, u32[]{:S(2)}) %collective-permute-start.38) | collective-permute-done | bytes 524320 | tf_op jit(solution)/shard_map/ppermute | solution.py:76
  284.3 7.5 %collective-permute-done.73 = f32[256,128]{1,0:T(8,128)S(1)} collective-permute-done((f32[256,128]{1,0:T(8,128)S(1)}, f32[256,128]{1,0:T(8,128)S(1)}, u32[]{:S(2)}, u32[]{:S(2)}) %collective-permute-start.73) | collective-permute-done | bytes 131104 | tf_op jit(solution)/shard_map/ppermute | solution.py:76
  314.0 11.7 %collective-permute-done.57.refs_1_ = f32[1024,128]{1,0:T(8,128)S(1)} collective-permute-done((f32[1024,128]{1,0:T(8,128)S(1)}, f32[1024,128]{1,0:T(8,128)S(1)}, u32[]{:S(2)}, u32[]{:S(2)}) %collective-permute-start.57) | collective-permute-done | bytes 524320 | tf_op jit(solution)/shard_map/ppermute | solution.py:76
  325.8 7.1 %older.3 = (f32[256,128]{1,0:T(8,128)}, f32[256,128]{1,0:T(8,128)}) custom-call(s32[16]{0:T(128)} %stack.73.meta_ref, f32[6,256,4096]{2,1,0:T(8,128)} %lower_ref.19, f32[256,128]{1,0:T(8,128)} %get-tuple-element.60.refs_0_, f32[256,128]{1,0:T(8,128)} %get-tuple-element.61.refs_1_, f32[1024,128]{1,0:T(8,128)} %copy-done.4, f32[1024,128]{1,0:T(8,128)} %copy-done.8, ...), custom_call_target="tpu_custom_call" | custom-call | tf_op jit(solution)/shard_map/older/pallas_call | solution.py:245
  332.9 8.7 %shard_map.80 = (f32[1024,128]{1,0:T(8,128)}, f32[1024,128]{1,0:T(8,128)}, f32[1024,128]{1,0:T(8,128)}, f32[1024,128]{1,0:T(8,128)}) custom-call(s32[16]{0:T(128)} %stack.73.meta_ref, f32[4,4096,256]{2,1,0:T(8,128)} %diag_ref.15, f32[6,256,4096]{2,1,0:T(8,128)} %lower_ref.19, f32[256,128]{1,0:T(8,128)} %get-tuple-element.76.pending_ref, ...), custom_call_target="tpu_custom_call" | custom-call | tf_op jit(solution)/shard_map/pallas_call | solution.py:207
  342.9 8.9 %shard_map.78 = (f32[1024,128]{1,0:T(8,128)}, f32[1024,128]{1,0:T(8,128)}, f32[1024,128]{1,0:T(8,128)}, f32[1024,128]{1,0:T(8,128)}) custom-call(s32[16]{0:T(128)} %stack.73.meta_ref, f32[4,4096,256]{2,1,0:T(8,128)} %diag_ref.15, f32[6,256,4096]{2,1,0:T(8,128)} %lower_ref.19, f32[256,128]{1,0:T(8,128)} %get-tuple-element.66.pending_ref, ...), custom_call_target="tpu_custom_call" | custom-call | tf_op jit(solution)/shard_map/pallas_call | solution.py:207
  356.7 10.6 %collective-permute-done.80 = f32[1024,128]{1,0:T(8,128)S(1)} collective-permute-done((f32[1024,128]{1,0:T(8,128)S(1)}, f32[1024,128]{1,0:T(8,128)S(1)}, u32[]{:S(2)}, u32[]{:S(2)}) %collective-permute-start.80) | collective-permute-done | bytes 524320 | tf_op jit(solution)/shard_map/ppermute | solution.py:76
  371.9 5.9 %collective-permute-done.62 = f32[1024,128]{1,0:T(8,128)S(1)} collective-permute-done((f32[1024,128]{1,0:T(8,128)S(1)}, f32[1024,128]{1,0:T(8,128)S(1)}, u32[]{:S(2)}, u32[]{:S(2)}) %collective-permute-start.62) | collective-permute-done | bytes 524320 | tf_op jit(solution)/shard_map/ppermute | solution.py:76
  (285 shorter events, 180.2 us)
Async XLA Ops:
  43.2 17.7 %collective-permute-start = (f32[1024,128]{1,0:T(8,128)}, f32[1024,128]{1,0:T(8,128)S(1)}, u32[]{:S(2)}, u32[]{:S(2)}) collective-permute-start(f32[1024,128]{1,0:T(8,128)} %get-tuple-element.44), channel_id=1, source_target_pairs={{0,1},{1,0},{2,3},{3,2},{4,5},{5,4},{6,7},{7,6},{8,9},{9,8},{10,11... | collective-permute-start | bytes 1572872 | tf_op jit(solution)/shard_map/ppermute | solution.py:76
  44.5 22.5 %collective-permute-start.2 = (f32[1024,128]{1,0:T(8,128)S(1)}, f32[1024,128]{1,0:T(8,128)S(1)}, u32[]{:S(2)}, u32[]{:S(2)}) collective-permute-start(f32[1024,128]{1,0:T(8,128)S(1)} %add.246), channel_id=1, source_target_pairs={{0,2},{1,3},{2,0},{3,1},{4,6},{5,7},{6,4},{7,5},{8,10},{9,11},{10,... | collective-permute-start | bytes 1572872 | tf_op jit(solution)/shard_map/ppermute | solution.py:76
  73.1 15.8 %collective-permute-start.25 = (f32[256,128]{1,0:T(8,128)S(1)}, f32[256,128]{1,0:T(8,128)S(1)}, u32[]{:S(2)}, u32[]{:S(2)}) collective-permute-start(f32[256,128]{1,0:T(8,128)S(1)} %fusion.27), channel_id=1, source_target_pairs={{0,8},{1,9},{2,10},{3,11},{4,12},{5,13},{6,14},{7,15},{8,0},{9,1},... | collective-permute-start | bytes 393224 | tf_op jit(solution)/shard_map/ppermute | solution.py:76
  77.6 16.9 %collective-permute-start.4 = (f32[256,128]{1,0:T(8,128)S(1)}, f32[256,128]{1,0:T(8,128)S(1)}, u32[]{:S(2)}, u32[]{:S(2)}) collective-permute-start(f32[256,128]{1,0:T(8,128)S(1)} %get-tuple-element.116), channel_id=1, source_target_pairs={{0,8},{1,9},{2,10},{3,11},{4,12},{5,13},{6,14},{7,15},{8,0},{9,1},... | collective-permute-start | bytes 393224 | tf_op jit(solution)/shard_map/ppermute | solution.py:76
  89.0 19.7 %collective-permute-start.27 = (f32[1024,128]{1,0:T(8,128)S(1)}, f32[1024,128]{1,0:T(8,128)S(1)}, u32[]{:S(2)}, u32[]{:S(2)}) collective-permute-start(f32[1024,128]{1,0:T(8,128)S(1)} %pad_maximum_fusion.1.refs_8_.refs_0_), channel_id=1, source_target_pairs={{0,2},{1,3},{2,0},{3,1},{4,6},{5,7},{6,4},{7,5},{8,10},{9,11},{10,... | collective-permute-start | bytes 1572872 | tf_op jit(solution)/shard_map/ppermute | solution.py:76
  109.1 22.1 %collective-permute-start.10 = (f32[1024,128]{1,0:T(8,128)S(1)}, f32[1024,128]{1,0:T(8,128)}, u32[]{:S(2)}, u32[]{:S(2)}) collective-permute-start(f32[1024,128]{1,0:T(8,128)S(1)} %pad_maximum_fusion.refs_0_.refs_4_), channel_id=1, source_target_pairs={{0,1},{1,0},{2,3},{3,2},{4,5},{5,4},{6,7},{7,6},{8,9},{9,8},{10,11... | collective-permute-start | bytes 1572872 | tf_op jit(solution)/shard_map/ppermute | solution.py:76
  142.4 17.8 %collective-permute-start.12 = (f32[1024,128]{1,0:T(8,128)}, f32[1024,128]{1,0:T(8,128)S(1)}, u32[]{:S(2)}, u32[]{:S(2)}) collective-permute-start(f32[1024,128]{1,0:T(8,128)} %get-tuple-element.48), channel_id=1, source_target_pairs={{0,1},{1,0},{2,3},{3,2},{4,5},{5,4},{6,7},{7,6},{8,9},{9,8},{10,11... | collective-permute-start | bytes 1572872 | tf_op jit(solution)/shard_map/ppermute | solution.py:76
  143.5 22.5 %collective-permute-start.14 = (f32[1024,128]{1,0:T(8,128)S(1)}, f32[1024,128]{1,0:T(8,128)S(1)}, u32[]{:S(2)}, u32[]{:S(2)}) collective-permute-start(f32[1024,128]{1,0:T(8,128)S(1)} %add.252), channel_id=1, source_target_pairs={{0,2},{1,3},{2,0},{3,1},{4,6},{5,7},{6,4},{7,5},{8,10},{9,11},{10,... | collective-permute-start | bytes 1572872 | tf_op jit(solution)/shard_map/ppermute | solution.py:76
  174.3 17.1 %collective-permute-start.16 = (f32[256,128]{1,0:T(8,128)S(1)}, f32[256,128]{1,0:T(8,128)S(1)}, u32[]{:S(2)}, u32[]{:S(2)}) collective-permute-start(f32[256,128]{1,0:T(8,128)S(1)} %get-tuple-element.106), channel_id=1, source_target_pairs={{0,8},{1,9},{2,10},{3,11},{4,12},{5,13},{6,14},{7,15},{8,0},{9,1},... | collective-permute-start | bytes 393224 | tf_op jit(solution)/shard_map/ppermute | solution.py:76
  184.6 21.5 %collective-permute-start.51 = (f32[1024,128]{1,0:T(8,128)S(1)}, f32[1024,128]{1,0:T(8,128)S(1)}, u32[]{:S(2)}, u32[]{:S(2)}) collective-permute-start(f32[1024,128]{1,0:T(8,128)S(1)} %pad_maximum_fusion.3.refs_6_.refs_0_), channel_id=1, source_target_pairs={{0,2},{1,3},{2,0},{3,1},{4,6},{5,7},{6,4},{7,5},{8,10},{9,11},{10,... | collective-permute-start | bytes 1572872 | tf_op jit(solution)/shard_map/ppermute | solution.py:76
  206.0 22.4 %collective-permute-start.52 = (f32[1024,128]{1,0:T(8,128)S(1)}, f32[1024,128]{1,0:T(8,128)S(1)}, u32[]{:S(2)}, u32[]{:S(2)}) collective-permute-start(f32[1024,128]{1,0:T(8,128)S(1)} %pad_maximum_fusion.3.refs_6_.refs_0_), channel_id=1, source_target_pairs={{0,1},{1,0},{2,3},{3,2},{4,5},{5,4},{6,7},{7,6},{8,9},{9,8},{10,11... | collective-permute-start | bytes 1572872 | tf_op jit(solution)/shard_map/ppermute | solution.py:76
  206.0 22.4 %collective-permute-start.53 = (f32[1024,128]{1,0:T(8,128)S(1)}, f32[1024,128]{1,0:T(8,128)S(1)}, u32[]{:S(2)}, u32[]{:S(2)}) collective-permute-start(f32[1024,128]{1,0:T(8,128)S(1)} %collective-permute-done.51.refs_7_.refs_1_), channel_id=1, source_target_pairs={{0,1},{1,0},{2,3},{3,2},{4,5},{5,4},{6,7},{7,6},{8,9},{9,8},{10,11... | collective-permute-start | bytes 1572872 | tf_op jit(solution)/shard_map/ppermute | solution.py:76
  206.5 32.0 %collective-permute-start.34 = (f32[1024,128]{1,0:T(8,128)S(1)}, f32[1024,128]{1,0:T(8,128)}, u32[]{:S(2)}, u32[]{:S(2)}) collective-permute-start(f32[1024,128]{1,0:T(8,128)S(1)} %pad_maximum_fusion.2.refs_0_.refs_2_), channel_id=1, source_target_pairs={{0,1},{1,0},{2,3},{3,2},{4,5},{5,4},{6,7},{7,6},{8,9},{9,8},{10,11... | collective-permute-start | bytes 1572872 | tf_op jit(solution)/shard_map/ppermute | solution.py:76
  218.3 20.2 %collective-permute-start.35 = (f32[1024,128]{1,0:T(8,128)S(1)}, f32[1024,128]{1,0:T(8,128)}, u32[]{:S(2)}, u32[]{:S(2)}) collective-permute-start(f32[1024,128]{1,0:T(8,128)S(1)} %collective-permute-done.33.refs_1_.refs_3_), channel_id=1, source_target_pairs={{0,1},{1,0},{2,3},{3,2},{4,5},{5,4},{6,7},{7,6},{8,9},{9,8},{10,11... | collective-permute-start | bytes 1572872 | tf_op jit(solution)/shard_map/ppermute | solution.py:76
  249.6 17.8 %collective-permute-start.36 = (f32[1024,128]{1,0:T(8,128)}, f32[1024,128]{1,0:T(8,128)S(1)}, u32[]{:S(2)}, u32[]{:S(2)}) collective-permute-start(f32[1024,128]{1,0:T(8,128)} %get-tuple-element.57), channel_id=1, source_target_pairs={{0,1},{1,0},{2,3},{3,2},{4,5},{5,4},{6,7},{7,6},{8,9},{9,8},{10,11... | collective-permute-start | bytes 1572872 | tf_op jit(solution)/shard_map/ppermute | solution.py:76
  250.8 22.6 %collective-permute-start.38 = (f32[1024,128]{1,0:T(8,128)S(1)}, f32[1024,128]{1,0:T(8,128)S(1)}, u32[]{:S(2)}, u32[]{:S(2)}) collective-permute-start(f32[1024,128]{1,0:T(8,128)S(1)} %add.267), channel_id=1, source_target_pairs={{0,2},{1,3},{2,0},{3,1},{4,6},{5,7},{6,4},{7,5},{8,10},{9,11},{10,... | collective-permute-start | bytes 1572872 | tf_op jit(solution)/shard_map/ppermute | solution.py:76
  281.7 17.1 %collective-permute-start.40 = (f32[256,128]{1,0:T(8,128)S(1)}, f32[256,128]{1,0:T(8,128)S(1)}, u32[]{:S(2)}, u32[]{:S(2)}) collective-permute-start(f32[256,128]{1,0:T(8,128)S(1)} %get-tuple-element.90), channel_id=1, source_target_pairs={{0,8},{1,9},{2,10},{3,11},{4,12},{5,13},{6,14},{7,15},{8,0},{9,1},... | collective-permute-start | bytes 393224 | tf_op jit(solution)/shard_map/ppermute | solution.py:76
  291.8 21.6 %collective-permute-start.75 = (f32[1024,128]{1,0:T(8,128)S(1)}, f32[1024,128]{1,0:T(8,128)S(1)}, u32[]{:S(2)}, u32[]{:S(2)}) collective-permute-start(f32[1024,128]{1,0:T(8,128)S(1)} %pad_maximum_fusion.5.refs_0_), channel_id=1, source_target_pairs={{0,2},{1,3},{2,0},{3,1},{4,6},{5,7},{6,4},{7,5},{8,10},{9,11},{10,... | collective-permute-start | bytes 1572872 | tf_op jit(solution)/shard_map/ppermute | solution.py:76
  313.4 19.5 %collective-permute-start.76 = (f32[1024,128]{1,0:T(8,128)S(1)}, f32[1024,128]{1,0:T(8,128)}, u32[]{:S(2)}, u32[]{:S(2)}) collective-permute-start(f32[1024,128]{1,0:T(8,128)S(1)} %pad_maximum_fusion.5.refs_0_), channel_id=1, source_target_pairs={{0,1},{1,0},{2,3},{3,2},{4,5},{5,4},{6,7},{7,6},{8,9},{9,8},{10,11... | collective-permute-start | bytes 1572872 | tf_op jit(solution)/shard_map/ppermute | solution.py:76
  313.4 19.5 %collective-permute-start.77 = (f32[1024,128]{1,0:T(8,128)S(1)}, f32[1024,128]{1,0:T(8,128)}, u32[]{:S(2)}, u32[]{:S(2)}) collective-permute-start(f32[1024,128]{1,0:T(8,128)S(1)} %collective-permute-done.75.refs_1_), channel_id=1, source_target_pairs={{0,1},{1,0},{2,3},{3,2},{4,5},{5,4},{6,7},{7,6},{8,9},{9,8},{10,11... | collective-permute-start | bytes 1572872 | tf_op jit(solution)/shard_map/ppermute | solution.py:76
  314.0 28.1 %collective-permute-start.58 = (f32[1024,128]{1,0:T(8,128)S(1)}, f32[1024,128]{1,0:T(8,128)S(1)}, u32[]{:S(2)}, u32[]{:S(2)}) collective-permute-start(f32[1024,128]{1,0:T(8,128)S(1)} %pad_maximum_fusion.4.refs_0_), channel_id=1, source_target_pairs={{0,1},{1,0},{2,3},{3,2},{4,5},{5,4},{6,7},{7,6},{8,9},{9,8},{10,11... | collective-permute-start | bytes 1572872 | tf_op jit(solution)/shard_map/ppermute | solution.py:76
  325.8 16.3 %collective-permute-start.59 = (f32[1024,128]{1,0:T(8,128)S(1)}, f32[1024,128]{1,0:T(8,128)}, u32[]{:S(2)}, u32[]{:S(2)}) collective-permute-start(f32[1024,128]{1,0:T(8,128)S(1)} %collective-permute-done.57.refs_1_), channel_id=1, source_target_pairs={{0,1},{1,0},{2,3},{3,2},{4,5},{5,4},{6,7},{7,6},{8,9},{9,8},{10,11... | collective-permute-start | bytes 1572872 | tf_op jit(solution)/shard_map/ppermute | solution.py:76
  354.1 17.9 %collective-permute-start.60 = (f32[1024,128]{1,0:T(8,128)}, f32[1024,128]{1,0:T(8,128)S(1)}, u32[]{:S(2)}, u32[]{:S(2)}) collective-permute-start(f32[1024,128]{1,0:T(8,128)} %get-tuple-element.68), channel_id=1, source_target_pairs={{0,1},{1,0},{2,3},{3,2},{4,5},{5,4},{6,7},{7,6},{8,9},{9,8},{10,11... | collective-permute-start | bytes 1572872 | tf_op jit(solution)/shard_map/ppermute | solution.py:76
  355.2 22.6 %collective-permute-start.62 = (f32[1024,128]{1,0:T(8,128)S(1)}, f32[1024,128]{1,0:T(8,128)S(1)}, u32[]{:S(2)}, u32[]{:S(2)}) collective-permute-start(f32[1024,128]{1,0:T(8,128)S(1)} %add.279), channel_id=1, source_target_pairs={{0,2},{1,3},{2,0},{3,1},{4,6},{5,7},{6,4},{7,5},{8,10},{9,11},{10,... | collective-permute-start | bytes 1572872 | tf_op jit(solution)/shard_map/ppermute | solution.py:76
  (97 other events, 1289.6 us)
where the time goes:
time: 393 us; the launch traced here: 392 us
  waiting for transfers between devices  180 us (46%)
  starting transfers between devices  88.5 us (23%)
  Pallas kernels  80.3 us (20%)
  local copies, waits for them, and re-layouts  26.2 us (7%)
  other arithmetic  11.4 us (3%)
  between operations  4.67 us (1%)
    ppermute x84, waiting for transfers between devices, send(): return lax.ppermute(value, COL, self.shift(dz, dy, dc))  180 us
    ppermute x84, starting transfers between devices, send(): return lax.ppermute(value, COL, self.shift(dz, dy, dc))  88.5 us
    pallas_call x8, Pallas kernels, section_product(): pl.pallas_call(functools.partial(section_kernel, sec_idx, pair, subs), ou...  63.2 us
    pallas_call x2, Pallas kernels, older_product(): pl.pallas_call(functools.partial(older_kernel, pairs, subs, chunks), out_...  17.1 us
    unnamed x78, local copies, waits for them, and re-layouts  9.91 us
  transfers between devices with their start and end apart: 84, of which 31 were waited for; matrix products, arithmetic and copies ran while one was open for 3% of the time, Pallas kernels for 19%

commit v1 on v0

--- a/solution.py
+++ b/solution.py
@@ -213,6 +213,65 @@
     )(meta, diag_inverse, lower_pairs, pending, *pieces)
 
 
+def feature_kernel(sections, sec, meta_ref, offsets_ref, ids_ref, table_ref, width_ref, path_ref, *outs):
+    features = table_ref.shape[0]
+    owned, lanes = outs[0].shape
+    first = meta_ref[meta_ref.shape[0] - 1]
+    chunks = offsets_ref.shape[0]
+    lane = lax.broadcasted_iota(jnp.int32, (features, lanes), 1)
+    one_lane = lax.broadcasted_iota(jnp.int32, (1, lanes), 1)
+    last = path_ref.shape[1] // lanes - 1
+    snaps = []
+    for m in range(chunks):
+        block = jnp.minimum(offsets_ref[m] // lanes, last)
+        inside = offsets_ref[m] - block * lanes
+        here = path_ref[:, pl.ds(pl.multiple_of(block * lanes, lanes), lanes)]
+        after = path_ref[:, pl.ds(pl.multiple_of(jnp.minimum(block + 1, last) * lanes, lanes), lanes)]
+        turn = (lanes - inside) % lanes
+        snap = jnp.where(lane < lanes - inside, pltpu.roll(here, turn, 1), pltpu.roll(after, turn, 1))
+        snaps.append((snap, jnp.sum(snap * snap, axis=0, keepdims=True)))
+    for at, sec_idx in enumerate(sections):
+        for group in range(owned // lanes):
+            base = sec_idx * sec + first + group * lanes
+
+            def pick(i, carry):
+                centers, rates = carry
+                number = ids_ref[base + i]
+                block = number // lanes
+                turn = (i - number % lanes + lanes) % lanes
+                column = table_ref[:, pl.ds(pl.multiple_of(block * lanes, lanes), lanes)]
+                centers = jnp.where(lane == i, pltpu.roll(column, turn, 1), centers)
+                rates = jnp.where(one_lane == i, pltpu.roll(width_ref[pl.ds(block, 1), :], turn, 1), rates)
+                return centers, rates
+
+            zero = jnp.zeros((features, lanes), jnp.float32)
+            centers, rates = lax.fori_loop(0, lanes, pick, (zero, zero[:1]), unroll=8)
+            pad = lanes - features
+            flat = jnp.concatenate([centers, jnp.broadcast_to(rates, (pad, lanes))], axis=0).T
+            centers, rates = flat[:, :features], flat[:, features : features + 1]
+            center_sq = jnp.sum(centers * centers, axis=1, keepdims=True)
+            for m, (snap, snap_sq) in enumerate(snaps):
+                cross = jnp.dot(
+                    centers, snap, precision=lax.Precision.HIGHEST, preferred_element_type=jnp.float32
+                )
+                dist = snap_sq + center_sq - 2.0 * cross
+                outs[at * chunks + m][pl.ds(group * lanes, lanes), :] = jnp.exp(-rates * dist / features)
+
+
+def features_of(meta, offsets, landmark_ids, landmarks, inv_width, trajectory, owned, sec, sections):
+    chunks = offsets.shape[0]
+    smem = pl.BlockSpec(memory_space=pltpu.SMEM)
+    vmem = pl.BlockSpec(memory_space=pltpu.VMEM)
+    out = pl.pallas_call(
+        functools.partial(feature_kernel, sections, sec),
+        out_shape=[jax.ShapeDtypeStruct((owned, BATCH), jnp.float32)] * (chunks * len(sections)),
+        in_specs=[smem, smem, smem, vmem, vmem, vmem],
+        out_specs=[vmem] * (chunks * len(sections)),
+        name="features",
+    )(meta, offsets, landmark_ids, landmarks.T, inv_width.reshape(-1, BATCH), trajectory.T)
+    return [out[at * chunks : (at + 1) * chunks] for at in range(len(sections))]
+
+
 def older_kernel(pairs, subs, chunks, meta_ref, lower_ref, *refs):
     count = len(pairs)
     pendings, refs = refs[: count * chunks], refs[count * chunks :]
@@ -261,7 +320,6 @@
     nsec = diag_inverse.shape[0]
     sec = diag_inverse.shape[1]
     owned = diag_inverse.shape[2]
-    features = landmarks.shape[1]
     outer, inner, cores = grid.extents
     me = lax.axis_index(COL)
     place = grid.split(me)
@@ -278,20 +336,17 @@
 
     to_z, to_sub = coordinates(grid.moved)
     from_z, from_sub = coordinates(grid.back)
-    meta = jnp.stack(to_z + from_z + to_sub + from_sub).astype(jnp.int32)
-
-    own_ids = lax.dynamic_slice_in_dim(landmark_ids.reshape(nsec, sec), first, owned, 1).reshape(-1)
-    centers = jnp.take(landmarks, own_ids, axis=0)
-    rates = jnp.take(inv_width, own_ids)
-    center_sq = jnp.sum(centers * centers, axis=1)[:, None]
+    meta = jnp.stack(to_z + from_z + to_sub + from_sub + [first]).astype(jnp.int32)
+
     chunks = offsets.shape[0]
-    pending = []
-    for m in range(chunks):
-        snap = lax.dynamic_slice_in_dim(trajectory, offsets[m], BATCH, 0)
-        cross = jnp.dot(centers, snap.T, precision=lax.Precision.HIGHEST, preferred_element_type=jnp.float32)
-        dist = jnp.sum(snap * snap, axis=1)[None, :] + center_sq - 2.0 * cross
-        kernel = jnp.exp(-rates[:, None] * dist / features)
-        pending.append([kernel[s * owned : (s + 1) * owned] for s in range(nsec)])
+
+    def features_in(sections):
+        return features_of(
+            meta, offsets, landmark_ids, landmarks, inv_width, trajectory, owned, sec, tuple(sections)
+        )
+
+    begin = features_in([0])[0]
+    pending = [[begin[m]] + [None] * (nsec - 1) for m in range(chunks)]
 
     cut = lambda arr, i: arr[i * owned : (i + 1) * owned]
 
@@ -337,6 +392,10 @@
             pieces = tuple(plane + [one for row in across for one in row])
 
     def older_steps():
+        for sec_idx, row in enumerate(features_in(range(1, nsec)), 1):
+            for m in range(chunks):
+                pending[m][sec_idx] = row[m]
+        yield
         for sec_idx in range(1, nsec - 1):
             later = range(sec_idx + 1, nsec)
             pairs = [s * (s - 1) // 2 + sec_idx - 1 for s in later]
@@ -367,7 +426,7 @@
             at = sec_idx * STEPS + step
             lag = 0.5 if 0 < at < 5 else 1.5
             keyed += [(at + m * lag, at, (m, sec_idx, step)) for m in range(chunks)]
-        if 0 < sec_idx < nsec - 1:
+        if sec_idx < nsec - 1:
             at = sec_idx * STEPS + 1
             keyed.append((at + 1.5 * (chunks - 1), at + 1, (chunks, sec_idx, 0)))
     return [entry for _, _, entry in sorted(keyed)]

time: 393 us -> 395 us (level)
  Pallas kernels: 80.3 us -> 110 us
  local copies, waits for them, and re-layouts: 26.2 us -> 3.72 us
  between operations: 4.67 us -> 0.63 us
    pallas_call x0 -> x2, Pallas kernels: none -> 30 us  [features_of(): pl.pallas_call(functools.partial(feature_kernel, sections, sec), out_shap...]
    gather x2 -> x0, local copies, waits for them, and re-layouts: 12.4 us -> none  [the longest x1 6.23 us: body(): centers = jnp.take(landmarks, own_ids, axis=0)]
    unnamed x78 -> x60, local copies, waits for them, and re-layouts: 9.91 us -> 2.89 us
  transfers between devices with their start and end apart: 84 -> 84, of which waited for: 31 -> 31; matrix products, arithmetic and copies ran while one was open for 3% -> 3% of each run, Pallas kernels for 19% -> 24%
where the time goes in v1:
time: 395 us; the launch traced here: 394 us
  waiting for transfers between devices  180 us (46%)
  Pallas kernels  110 us (28%)
  starting transfers between devices  88.1 us (22%)
  other arithmetic  11 us (3%)
    ppermute x84, waiting for transfers between devices, send(): return lax.ppermute(value, COL, self.shift(dz, dy, dc))  180 us
    ppermute x84, starting transfers between devices, send(): return lax.ppermute(value, COL, self.shift(dz, dy, dc))  88.1 us
    pallas_call x8, Pallas kernels, section_product(): pl.pallas_call(functools.partial(section_kernel, sec_idx, pair, subs), ou...  63.2 us
    pallas_call x2, Pallas kernels, features_of(): pl.pallas_call(functools.partial(feature_kernel, sections, sec), out_shap...  30 us
    pallas_call x2, Pallas kernels, older_product(): pl.pallas_call(functools.partial(older_kernel, pairs, subs, chunks), out_...  17.1 us
  transfers between devices with their start and end apart: 84, of which 31 were waited for; matrix products, arithmetic and copies ran while one was open for 3% of the time, Pallas kernels for 24%

profile of v1, /device:TPU:0, one launch (start us, length us, event | category | flops | bytes accessed | tf_op | source)
XLA Modules:
  0.0 394.1 jit_solution(15119524878669095902)
XLA Ops:
  0.6 9.0 %features.2 = (f32[256,128]{1,0:T(8,128)}, f32[256,128]{1,0:T(8,128)}) custom-call(s32[17]{0:T(128)} %stack.77.meta_ref, s32[2]{0:T(128)} %offsets_ref.3, s32[16384]{0:T(1024)} %ids_ref.3, f32[64,16384]{1,0:T(8,128)} %bitcast.22, f32[128,128]{1,0:T(8,128)} %bitcast.32, f32[64,1024]{1,0:T(8,128)} %bitcast.30), custom_call_target="tpu_custom_call" | custom-call | tf_op jit(solution)/shard_map/features/pallas_call | solution.py:265
  26.5 10.1 %collective-permute-done.20 = f32[1024,128]{1,0:T(8,128)S(1)} collective-permute-done((f32[1024,128]{1,0:T(8,128)S(1)}, f32[1024,128]{1,0:T(8,128)S(1)}, u32[]{:S(2)}, u32[]{:S(2)}) %collective-permute-start.20) | collective-permute-done | bytes 524320 | tf_op jit(solution)/shard_map/ppermute | solution.py:76
  41.5 6.0 %collective-permute-done.2 = f32[1024,128]{1,0:T(8,128)S(1)} collective-permute-done((f32[1024,128]{1,0:T(8,128)S(1)}, f32[1024,128]{1,0:T(8,128)S(1)}, u32[]{:S(2)}, u32[]{:S(2)}) %collective-permute-start.2) | collective-permute-done | bytes 524320 | tf_op jit(solution)/shard_map/ppermute | solution.py:76
  61.7 7.9 %collective-permute-done.25 = f32[256,128]{1,0:T(8,128)S(1)} collective-permute-done((f32[256,128]{1,0:T(8,128)S(1)}, f32[256,128]{1,0:T(8,128)S(1)}, u32[]{:S(2)}, u32[]{:S(2)}) %collective-permute-start.25) | collective-permute-done | bytes 131104 | tf_op jit(solution)/shard_map/ppermute | solution.py:76
  89.8 11.8 %collective-permute-done.9.refs_1_.refs_5_ = f32[1024,128]{1,0:T(8,128)S(1)} collective-permute-done((f32[1024,128]{1,0:T(8,128)S(1)}, f32[1024,128]{1,0:T(8,128)S(1)}, u32[]{:S(2)}, u32[]{:S(2)}) %collective-permute-start.9) | collective-permute-done | bytes 524320 | tf_op jit(solution)/shard_map/ppermute | solution.py:76
  101.6 21.0 %features.3 = (f32[256,128]{1,0:T(8,128)}, f32[256,128]{1,0:T(8,128)}, f32[256,128]{1,0:T(8,128)}, f32[256,128]{1,0:T(8,128)}, f32[256,128]{1,0:T(8,128)}, /*index=5*/f32[256,128]{1,0:T(8,128)}) custom-call(s32[17]{0:T(128)} %stack.77.meta_ref, s32[2]{0:T(128)} %offsets_ref.3, s32[16384]{0:T(1024)} %ids_ref.3, f32[64,16384]{1,0:T(8,128)} %bitcast.23, ...), custom_call_target="tpu_custom_call" | custom-call | tf_op jit(solution)/shard_map/features/pallas_call | solution.py:265
  123.7 8.7 %shard_map.77 = (f32[1024,128]{1,0:T(8,128)}, f32[1024,128]{1,0:T(8,128)}, f32[1024,128]{1,0:T(8,128)}, f32[1024,128]{1,0:T(8,128)}) custom-call(s32[17]{0:T(128)} %stack.77.meta_ref, f32[4,4096,256]{2,1,0:T(8,128)} %diag_ref.15, f32[6,256,4096]{2,1,0:T(8,128)} %lower_ref.19, f32[256,128]{1,0:T(8,128)} %get-tuple-element.77.pending_ref, ...), custom_call_target="tpu_custom_call" | custom-call | tf_op jit(solution)/shard_map/pallas_call | solution.py:207
  132.8 8.9 %shard_map.74 = (f32[1024,128]{1,0:T(8,128)}, f32[1024,128]{1,0:T(8,128)}, f32[1024,128]{1,0:T(8,128)}, f32[1024,128]{1,0:T(8,128)}) custom-call(s32[17]{0:T(128)} %stack.77.meta_ref, f32[4,4096,256]{2,1,0:T(8,128)} %diag_ref.15, f32[6,256,4096]{2,1,0:T(8,128)} %lower_ref.19, f32[256,128]{1,0:T(8,128)} %get-tuple-element.56.pending_ref, ...), custom_call_target="tpu_custom_call" | custom-call | tf_op jit(solution)/shard_map/pallas_call | solution.py:207
  146.6 10.6 %collective-permute-done.44 = f32[1024,128]{1,0:T(8,128)S(1)} collective-permute-done((f32[1024,128]{1,0:T(8,128)S(1)}, f32[1024,128]{1,0:T(8,128)S(1)}, u32[]{:S(2)}, u32[]{:S(2)}) %collective-permute-start.44) | collective-permute-done | bytes 524320 | tf_op jit(solution)/shard_map/ppermute | solution.py:76
  161.8 5.9 %collective-permute-done.14 = f32[1024,128]{1,0:T(8,128)S(1)} collective-permute-done((f32[1024,128]{1,0:T(8,128)S(1)}, f32[1024,128]{1,0:T(8,128)S(1)}, u32[]{:S(2)}, u32[]{:S(2)}) %collective-permute-start.14) | collective-permute-done | bytes 524320 | tf_op jit(solution)/shard_map/ppermute | solution.py:76
  178.2 8.3 %collective-permute-done.49 = f32[256,128]{1,0:T(8,128)S(1)} collective-permute-done((f32[256,128]{1,0:T(8,128)S(1)}, f32[256,128]{1,0:T(8,128)S(1)}, u32[]{:S(2)}, u32[]{:S(2)}) %collective-permute-start.49) | collective-permute-done | bytes 131104 | tf_op jit(solution)/shard_map/ppermute | solution.py:76
  208.4 11.8 %collective-permute-done.33.refs_1_.refs_3_ = f32[1024,128]{1,0:T(8,128)S(1)} collective-permute-done((f32[1024,128]{1,0:T(8,128)S(1)}, f32[1024,128]{1,0:T(8,128)S(1)}, u32[]{:S(2)}, u32[]{:S(2)}) %collective-permute-start.33) | collective-permute-done | bytes 524320 | tf_op jit(solution)/shard_map/ppermute | solution.py:76
  220.1 10.0 %older.2 = (f32[256,128]{1,0:T(8,128)}, f32[256,128]{1,0:T(8,128)}, f32[256,128]{1,0:T(8,128)}, f32[256,128]{1,0:T(8,128)}) custom-call(s32[17]{0:T(128)} %stack.77.meta_ref, f32[6,256,4096]{2,1,0:T(8,128)} %lower_ref.19, f32[256,128]{1,0:T(8,128)} %get-tuple-element.61.refs_0_, f32[256,128]{1,0:T(8,128)} %get-tuple-element.62.refs_1_, ...), custom_call_target="tpu_custom_call" | custom-call | tf_op jit(solution)/shard_map/older/pallas_call | solution.py:304
  231.2 8.7 %shard_map.79 = (f32[1024,128]{1,0:T(8,128)}, f32[1024,128]{1,0:T(8,128)}, f32[1024,128]{1,0:T(8,128)}, f32[1024,128]{1,0:T(8,128)}) custom-call(s32[17]{0:T(128)} %stack.77.meta_ref, f32[4,4096,256]{2,1,0:T(8,128)} %diag_ref.15, f32[6,256,4096]{2,1,0:T(8,128)} %lower_ref.19, f32[256,128]{1,0:T(8,128)} %get-tuple-element.87.pending_ref, ...), custom_call_target="tpu_custom_call" | custom-call | tf_op jit(solution)/shard_map/pallas_call | solution.py:207
  240.4 8.9 %shard_map.76 = (f32[1024,128]{1,0:T(8,128)}, f32[1024,128]{1,0:T(8,128)}, f32[1024,128]{1,0:T(8,128)}, f32[1024,128]{1,0:T(8,128)}) custom-call(s32[17]{0:T(128)} %stack.77.meta_ref, f32[4,4096,256]{2,1,0:T(8,128)} %diag_ref.15, f32[6,256,4096]{2,1,0:T(8,128)} %lower_ref.19, f32[256,128]{1,0:T(8,128)} %get-tuple-element.70.pending_ref, ...), custom_call_target="tpu_custom_call" | custom-call | tf_op jit(solution)/shard_map/pallas_call | solution.py:207
  254.1 10.6 %collective-permute-done.68 = f32[1024,128]{1,0:T(8,128)S(1)} collective-permute-done((f32[1024,128]{1,0:T(8,128)S(1)}, f32[1024,128]{1,0:T(8,128)S(1)}, u32[]{:S(2)}, u32[]{:S(2)}) %collective-permute-start.68) | collective-permute-done | bytes 524320 | tf_op jit(solution)/shard_map/ppermute | solution.py:76
  269.3 5.9 %collective-permute-done.38 = f32[1024,128]{1,0:T(8,128)S(1)} collective-permute-done((f32[1024,128]{1,0:T(8,128)S(1)}, f32[1024,128]{1,0:T(8,128)S(1)}, u32[]{:S(2)}, u32[]{:S(2)}) %collective-permute-start.38) | collective-permute-done | bytes 524320 | tf_op jit(solution)/shard_map/ppermute | solution.py:76
  286.1 7.6 %collective-permute-done.73 = f32[256,128]{1,0:T(8,128)S(1)} collective-permute-done((f32[256,128]{1,0:T(8,128)S(1)}, f32[256,128]{1,0:T(8,128)S(1)}, u32[]{:S(2)}, u32[]{:S(2)}) %collective-permute-start.73) | collective-permute-done | bytes 131104 | tf_op jit(solution)/shard_map/ppermute | solution.py:76
  315.9 11.8 %collective-permute-done.57.refs_1_ = f32[1024,128]{1,0:T(8,128)S(1)} collective-permute-done((f32[1024,128]{1,0:T(8,128)S(1)}, f32[1024,128]{1,0:T(8,128)S(1)}, u32[]{:S(2)}, u32[]{:S(2)}) %collective-permute-start.57) | collective-permute-done | bytes 524320 | tf_op jit(solution)/shard_map/ppermute | solution.py:76
  327.6 7.1 %older.3 = (f32[256,128]{1,0:T(8,128)}, f32[256,128]{1,0:T(8,128)}) custom-call(s32[17]{0:T(128)} %stack.77.meta_ref, f32[6,256,4096]{2,1,0:T(8,128)} %lower_ref.19, f32[256,128]{1,0:T(8,128)} %get-tuple-element.75.refs_0_, f32[256,128]{1,0:T(8,128)} %get-tuple-element.76.refs_1_, f32[1024,128]{1,0:T(8,128)} %copy-done.2, f32[1024,128]{1,0:T(8,128)} %copy-done.6, ...), custom_call_target="tpu_custom_call" | custom-call | tf_op jit(solution)/shard_map/older/pallas_call | solution.py:304
  334.8 8.7 %shard_map.80 = (f32[1024,128]{1,0:T(8,128)}, f32[1024,128]{1,0:T(8,128)}, f32[1024,128]{1,0:T(8,128)}, f32[1024,128]{1,0:T(8,128)}) custom-call(s32[17]{0:T(128)} %stack.77.meta_ref, f32[4,4096,256]{2,1,0:T(8,128)} %diag_ref.15, f32[6,256,4096]{2,1,0:T(8,128)} %lower_ref.19, f32[256,128]{1,0:T(8,128)} %get-tuple-element.92.pending_ref, ...), custom_call_target="tpu_custom_call" | custom-call | tf_op jit(solution)/shard_map/pallas_call | solution.py:207
  344.8 8.9 %shard_map.78 = (f32[1024,128]{1,0:T(8,128)}, f32[1024,128]{1,0:T(8,128)}, f32[1024,128]{1,0:T(8,128)}, f32[1024,128]{1,0:T(8,128)}) custom-call(s32[17]{0:T(128)} %stack.77.meta_ref, f32[4,4096,256]{2,1,0:T(8,128)} %diag_ref.15, f32[6,256,4096]{2,1,0:T(8,128)} %lower_ref.19, f32[256,128]{1,0:T(8,128)} %get-tuple-element.82.pending_ref, ...), custom_call_target="tpu_custom_call" | custom-call | tf_op jit(solution)/shard_map/pallas_call | solution.py:207
  358.5 10.6 %collective-permute-done.80 = f32[1024,128]{1,0:T(8,128)S(1)} collective-permute-done((f32[1024,128]{1,0:T(8,128)S(1)}, f32[1024,128]{1,0:T(8,128)S(1)}, u32[]{:S(2)}, u32[]{:S(2)}) %collective-permute-start.80) | collective-permute-done | bytes 524320 | tf_op jit(solution)/shard_map/ppermute | solution.py:76
  373.7 5.9 %collective-permute-done.62 = f32[1024,128]{1,0:T(8,128)S(1)} collective-permute-done((f32[1024,128]{1,0:T(8,128)S(1)}, f32[1024,128]{1,0:T(8,128)S(1)}, u32[]{:S(2)}, u32[]{:S(2)}) %collective-permute-start.62) | collective-permute-done | bytes 524320 | tf_op jit(solution)/shard_map/ppermute | solution.py:76
  (256 shorter events, 168.8 us)
Async XLA Ops:
  23.8 17.7 %collective-permute-start = (f32[1024,128]{1,0:T(8,128)}, f32[1024,128]{1,0:T(8,128)S(1)}, u32[]{:S(2)}, u32[]{:S(2)}) collective-permute-start(f32[1024,128]{1,0:T(8,128)} %get-tuple-element.53), channel_id=1, source_target_pairs={{0,1},{1,0},{2,3},{3,2},{4,5},{5,4},{6,7},{7,6},{8,9},{9,8},{10,11... | collective-permute-start | bytes 1572872 | tf_op jit(solution)/shard_map/ppermute | solution.py:76
  25.1 22.5 %collective-permute-start.2 = (f32[1024,128]{1,0:T(8,128)S(1)}, f32[1024,128]{1,0:T(8,128)S(1)}, u32[]{:S(2)}, u32[]{:S(2)}) collective-permute-start(f32[1024,128]{1,0:T(8,128)S(1)} %add.176), channel_id=1, source_target_pairs={{0,2},{1,3},{2,0},{3,1},{4,6},{5,7},{6,4},{7,5},{8,10},{9,11},{10,... | collective-permute-start | bytes 1572872 | tf_op jit(solution)/shard_map/ppermute | solution.py:76
  69.6 19.7 %collective-permute-start.27 = (f32[1024,128]{1,0:T(8,128)S(1)}, f32[1024,128]{1,0:T(8,128)S(1)}, u32[]{:S(2)}, u32[]{:S(2)}) collective-permute-start(f32[1024,128]{1,0:T(8,128)S(1)} %pad_maximum_fusion.1.refs_8_.refs_0_), channel_id=1, source_target_pairs={{0,2},{1,3},{2,0},{3,1},{4,6},{5,7},{6,4},{7,5},{8,10},{9,11},{10,... | collective-permute-start | bytes 1572872 | tf_op jit(solution)/shard_map/ppermute | solution.py:76
  89.2 33.4 %collective-permute-start.28 = (f32[1024,128]{1,0:T(8,128)S(1)}, f32[1024,128]{1,0:T(8,128)S(1)}, u32[]{:S(2)}, u32[]{:S(2)}) collective-permute-start(f32[1024,128]{1,0:T(8,128)S(1)} %pad_maximum_fusion.1.refs_8_.refs_0_), channel_id=1, source_target_pairs={{0,1},{1,0},{2,3},{3,2},{4,5},{5,4},{6,7},{7,6},{8,9},{9,8},{10,11... | collective-permute-start | bytes 1572872 | tf_op jit(solution)/shard_map/ppermute | solution.py:76
  89.2 33.4 %collective-permute-start.29 = (f32[1024,128]{1,0:T(8,128)S(1)}, f32[1024,128]{1,0:T(8,128)S(1)}, u32[]{:S(2)}, u32[]{:S(2)}) collective-permute-start(f32[1024,128]{1,0:T(8,128)S(1)} %collective-permute-done.27.refs_9_.refs_1_), channel_id=1, source_target_pairs={{0,1},{1,0},{2,3},{3,2},{4,5},{5,4},{6,7},{7,6},{8,9},{9,8},{10,11... | collective-permute-start | bytes 1572872 | tf_op jit(solution)/shard_map/ppermute | solution.py:76
  89.7 43.1 %collective-permute-start.10 = (f32[1024,128]{1,0:T(8,128)S(1)}, f32[1024,128]{1,0:T(8,128)}, u32[]{:S(2)}, u32[]{:S(2)}) collective-permute-start(f32[1024,128]{1,0:T(8,128)S(1)} %pad_maximum_fusion.refs_0_.refs_4_), channel_id=1, source_target_pairs={{0,1},{1,0},{2,3},{3,2},{4,5},{5,4},{6,7},{7,6},{8,9},{9,8},{10,11... | collective-permute-start | bytes 1572872 | tf_op jit(solution)/shard_map/ppermute | solution.py:76
  101.6 31.2 %collective-permute-start.11 = (f32[1024,128]{1,0:T(8,128)S(1)}, f32[1024,128]{1,0:T(8,128)}, u32[]{:S(2)}, u32[]{:S(2)}) collective-permute-start(f32[1024,128]{1,0:T(8,128)S(1)} %collective-permute-done.9.refs_1_.refs_5_), channel_id=1, source_target_pairs={{0,1},{1,0},{2,3},{3,2},{4,5},{5,4},{6,7},{7,6},{8,9},{9,8},{10,11... | collective-permute-start | bytes 1572872 | tf_op jit(solution)/shard_map/ppermute | solution.py:76
  143.9 17.9 %collective-permute-start.12 = (f32[1024,128]{1,0:T(8,128)}, f32[1024,128]{1,0:T(8,128)S(1)}, u32[]{:S(2)}, u32[]{:S(2)}) collective-permute-start(f32[1024,128]{1,0:T(8,128)} %get-tuple-element.58), channel_id=1, source_target_pairs={{0,1},{1,0},{2,3},{3,2},{4,5},{5,4},{6,7},{7,6},{8,9},{9,8},{10,11... | collective-permute-start | bytes 1572872 | tf_op jit(solution)/shard_map/ppermute | solution.py:76
  145.1 22.6 %collective-permute-start.14 = (f32[1024,128]{1,0:T(8,128)S(1)}, f32[1024,128]{1,0:T(8,128)S(1)}, u32[]{:S(2)}, u32[]{:S(2)}) collective-permute-start(f32[1024,128]{1,0:T(8,128)S(1)} %add.182), channel_id=1, source_target_pairs={{0,2},{1,3},{2,0},{3,1},{4,6},{5,7},{6,4},{7,5},{8,10},{9,11},{10,... | collective-permute-start | bytes 1572872 | tf_op jit(solution)/shard_map/ppermute | solution.py:76
  175.8 17.4 %collective-permute-start.16 = (f32[256,128]{1,0:T(8,128)S(1)}, f32[256,128]{1,0:T(8,128)S(1)}, u32[]{:S(2)}, u32[]{:S(2)}) collective-permute-start(f32[256,128]{1,0:T(8,128)S(1)} %get-tuple-element.114), channel_id=1, source_target_pairs={{0,8},{1,9},{2,10},{3,11},{4,12},{5,13},{6,14},{7,15},{8,0},{9,1},... | collective-permute-start | bytes 393224 | tf_op jit(solution)/shard_map/ppermute | solution.py:76
  186.6 21.2 %collective-permute-start.51 = (f32[1024,128]{1,0:T(8,128)S(1)}, f32[1024,128]{1,0:T(8,128)S(1)}, u32[]{:S(2)}, u32[]{:S(2)}) collective-permute-start(f32[1024,128]{1,0:T(8,128)S(1)} %pad_maximum_fusion.3.refs_6_.refs_0_), channel_id=1, source_target_pairs={{0,2},{1,3},{2,0},{3,1},{4,6},{5,7},{6,4},{7,5},{8,10},{9,11},{10,... | collective-permute-start | bytes 1572872 | tf_op jit(solution)/shard_map/ppermute | solution.py:76
  207.8 22.4 %collective-permute-start.52 = (f32[1024,128]{1,0:T(8,128)S(1)}, f32[1024,128]{1,0:T(8,128)S(1)}, u32[]{:S(2)}, u32[]{:S(2)}) collective-permute-start(f32[1024,128]{1,0:T(8,128)S(1)} %pad_maximum_fusion.3.refs_6_.refs_0_), channel_id=1, source_target_pairs={{0,1},{1,0},{2,3},{3,2},{4,5},{5,4},{6,7},{7,6},{8,9},{9,8},{10,11... | collective-permute-start | bytes 1572872 | tf_op jit(solution)/shard_map/ppermute | solution.py:76
  207.8 22.4 %collective-permute-start.53 = (f32[1024,128]{1,0:T(8,128)S(1)}, f32[1024,128]{1,0:T(8,128)S(1)}, u32[]{:S(2)}, u32[]{:S(2)}) collective-permute-start(f32[1024,128]{1,0:T(8,128)S(1)} %collective-permute-done.51.refs_7_.refs_1_), channel_id=1, source_target_pairs={{0,1},{1,0},{2,3},{3,2},{4,5},{5,4},{6,7},{7,6},{8,9},{9,8},{10,11... | collective-permute-start | bytes 1572872 | tf_op jit(solution)/shard_map/ppermute | solution.py:76
  208.3 32.0 %collective-permute-start.34 = (f32[1024,128]{1,0:T(8,128)S(1)}, f32[1024,128]{1,0:T(8,128)}, u32[]{:S(2)}, u32[]{:S(2)}) collective-permute-start(f32[1024,128]{1,0:T(8,128)S(1)} %pad_maximum_fusion.2.refs_0_.refs_2_), channel_id=1, source_target_pairs={{0,1},{1,0},{2,3},{3,2},{4,5},{5,4},{6,7},{7,6},{8,9},{9,8},{10,11... | collective-permute-start | bytes 1572872 | tf_op jit(solution)/shard_map/ppermute | solution.py:76
  220.1 20.2 %collective-permute-start.35 = (f32[1024,128]{1,0:T(8,128)S(1)}, f32[1024,128]{1,0:T(8,128)}, u32[]{:S(2)}, u32[]{:S(2)}) collective-permute-start(f32[1024,128]{1,0:T(8,128)S(1)} %collective-permute-done.33.refs_1_.refs_3_), channel_id=1, source_target_pairs={{0,1},{1,0},{2,3},{3,2},{4,5},{5,4},{6,7},{7,6},{8,9},{9,8},{10,11... | collective-permute-start | bytes 1572872 | tf_op jit(solution)/shard_map/ppermute | solution.py:76
  251.5 17.9 %collective-permute-start.36 = (f32[1024,128]{1,0:T(8,128)}, f32[1024,128]{1,0:T(8,128)S(1)}, u32[]{:S(2)}, u32[]{:S(2)}) collective-permute-start(f32[1024,128]{1,0:T(8,128)} %get-tuple-element.72), channel_id=1, source_target_pairs={{0,1},{1,0},{2,3},{3,2},{4,5},{5,4},{6,7},{7,6},{8,9},{9,8},{10,11... | collective-permute-start | bytes 1572872 | tf_op jit(solution)/shard_map/ppermute | solution.py:76
  252.6 22.6 %collective-permute-start.38 = (f32[1024,128]{1,0:T(8,128)S(1)}, f32[1024,128]{1,0:T(8,128)S(1)}, u32[]{:S(2)}, u32[]{:S(2)}) collective-permute-start(f32[1024,128]{1,0:T(8,128)S(1)} %add.194), channel_id=1, source_target_pairs={{0,2},{1,3},{2,0},{3,1},{4,6},{5,7},{6,4},{7,5},{8,10},{9,11},{10,... | collective-permute-start | bytes 1572872 | tf_op jit(solution)/shard_map/ppermute | solution.py:76
  283.6 17.1 %collective-permute-start.40 = (f32[256,128]{1,0:T(8,128)S(1)}, f32[256,128]{1,0:T(8,128)S(1)}, u32[]{:S(2)}, u32[]{:S(2)}) collective-permute-start(f32[256,128]{1,0:T(8,128)S(1)} %get-tuple-element.102), channel_id=1, source_target_pairs={{0,8},{1,9},{2,10},{3,11},{4,12},{5,13},{6,14},{7,15},{8,0},{9,1},... | collective-permute-start | bytes 393224 | tf_op jit(solution)/shard_map/ppermute | solution.py:76
  293.8 21.5 %collective-permute-start.75 = (f32[1024,128]{1,0:T(8,128)S(1)}, f32[1024,128]{1,0:T(8,128)S(1)}, u32[]{:S(2)}, u32[]{:S(2)}) collective-permute-start(f32[1024,128]{1,0:T(8,128)S(1)} %pad_maximum_fusion.5.refs_0_), channel_id=1, source_target_pairs={{0,2},{1,3},{2,0},{3,1},{4,6},{5,7},{6,4},{7,5},{8,10},{9,11},{10,... | collective-permute-start | bytes 1572872 | tf_op jit(solution)/shard_map/ppermute | solution.py:76
  315.3 19.5 %collective-permute-start.76 = (f32[1024,128]{1,0:T(8,128)S(1)}, f32[1024,128]{1,0:T(8,128)}, u32[]{:S(2)}, u32[]{:S(2)}) collective-permute-start(f32[1024,128]{1,0:T(8,128)S(1)} %pad_maximum_fusion.5.refs_0_), channel_id=1, source_target_pairs={{0,1},{1,0},{2,3},{3,2},{4,5},{5,4},{6,7},{7,6},{8,9},{9,8},{10,11... | collective-permute-start | bytes 1572872 | tf_op jit(solution)/shard_map/ppermute | solution.py:76
  315.3 19.5 %collective-permute-start.77 = (f32[1024,128]{1,0:T(8,128)S(1)}, f32[1024,128]{1,0:T(8,128)}, u32[]{:S(2)}, u32[]{:S(2)}) collective-permute-start(f32[1024,128]{1,0:T(8,128)S(1)} %collective-permute-done.75.refs_1_), channel_id=1, source_target_pairs={{0,1},{1,0},{2,3},{3,2},{4,5},{5,4},{6,7},{7,6},{8,9},{9,8},{10,11... | collective-permute-start | bytes 1572872 | tf_op jit(solution)/shard_map/ppermute | solution.py:76
  315.8 28.1 %collective-permute-start.58 = (f32[1024,128]{1,0:T(8,128)S(1)}, f32[1024,128]{1,0:T(8,128)S(1)}, u32[]{:S(2)}, u32[]{:S(2)}) collective-permute-start(f32[1024,128]{1,0:T(8,128)S(1)} %pad_maximum_fusion.4.refs_0_), channel_id=1, source_target_pairs={{0,1},{1,0},{2,3},{3,2},{4,5},{5,4},{6,7},{7,6},{8,9},{9,8},{10,11... | collective-permute-start | bytes 1572872 | tf_op jit(solution)/shard_map/ppermute | solution.py:76
  355.9 17.9 %collective-permute-start.60 = (f32[1024,128]{1,0:T(8,128)}, f32[1024,128]{1,0:T(8,128)S(1)}, u32[]{:S(2)}, u32[]{:S(2)}) collective-permute-start(f32[1024,128]{1,0:T(8,128)} %get-tuple-element.84), channel_id=1, source_target_pairs={{0,1},{1,0},{2,3},{3,2},{4,5},{5,4},{6,7},{7,6},{8,9},{9,8},{10,11... | collective-permute-start | bytes 1572872 | tf_op jit(solution)/shard_map/ppermute | solution.py:76
  357.0 22.6 %collective-permute-start.62 = (f32[1024,128]{1,0:T(8,128)S(1)}, f32[1024,128]{1,0:T(8,128)S(1)}, u32[]{:S(2)}, u32[]{:S(2)}) collective-permute-start(f32[1024,128]{1,0:T(8,128)S(1)} %add.206), channel_id=1, source_target_pairs={{0,2},{1,3},{2,0},{3,1},{4,6},{5,7},{6,4},{7,5},{8,10},{9,11},{10,... | collective-permute-start | bytes 1572872 | tf_op jit(solution)/shard_map/ppermute | solution.py:76
  (90 other events, 1270.2 us)

commit v2 on v1

--- a/solution.py
+++ b/solution.py
@@ -237,15 +237,15 @@
             def pick(i, carry):
                 centers, rates = carry
                 number = ids_ref[base + i]
-                block = number // lanes
-                turn = (i - number % lanes + lanes) % lanes
+                block = lax.shift_right_logical(number, lanes.bit_length() - 1)
+                turn = (i - number) & (lanes - 1)
                 column = table_ref[:, pl.ds(pl.multiple_of(block * lanes, lanes), lanes)]
                 centers = jnp.where(lane == i, pltpu.roll(column, turn, 1), centers)
                 rates = jnp.where(one_lane == i, pltpu.roll(width_ref[pl.ds(block, 1), :], turn, 1), rates)
                 return centers, rates
 
             zero = jnp.zeros((features, lanes), jnp.float32)
-            centers, rates = lax.fori_loop(0, lanes, pick, (zero, zero[:1]), unroll=8)
+            centers, rates = lax.fori_loop(0, lanes, pick, (zero, zero[:1]), unroll=16)
             pad = lanes - features
             flat = jnp.concatenate([centers, jnp.broadcast_to(rates, (pad, lanes))], axis=0).T
             centers, rates = flat[:, :features], flat[:, features : features + 1]
@@ -392,10 +392,11 @@
             pieces = tuple(plane + [one for row in across for one in row])
 
     def older_steps():
-        for sec_idx, row in enumerate(features_in(range(1, nsec)), 1):
-            for m in range(chunks):
-                pending[m][sec_idx] = row[m]
-        yield
+        for sections in feature_parts(nsec):
+            for sec_idx, row in zip(sections, features_in(sections)):
+                for m in range(chunks):
+                    pending[m][sec_idx] = row[m]
+            yield
         for sec_idx in range(1, nsec - 1):
             later = range(sec_idx + 1, nsec)
             pairs = [s * (s - 1) // 2 + sec_idx - 1 for s in later]
@@ -426,10 +427,17 @@
             at = sec_idx * STEPS + step
             lag = 0.5 if 0 < at < 5 else 1.5
             keyed += [(at + m * lag, at, (m, sec_idx, step)) for m in range(chunks)]
-        if sec_idx < nsec - 1:
+        if sec_idx == 0:
+            for part, at in zip(range(len(feature_parts(nsec))), (3.6, 4.6)):
+                keyed.append((at, at, (chunks, 0, part)))
+        elif sec_idx < nsec - 1:
             at = sec_idx * STEPS + 1
             keyed.append((at + 1.5 * (chunks - 1), at + 1, (chunks, sec_idx, 0)))
     return [entry for _, _, entry in sorted(keyed)]
+
+
+def feature_parts(nsec):
+    return [one for one in (list(range(1, min(2, nsec))), list(range(2, nsec))) if one]
 
 
 def solution(mesh):

time: 395 us -> 392 us (level)
    pallas_call x2 -> x3, Pallas kernels: 30 us -> 27.3 us  [features_of(): pl.pallas_call(functools.partial(feature_kernel, sections, sec), out_shap...]
where the time goes in v2:
time: 392 us
  waiting for transfers between devices  181 us (46%)
  Pallas kernels  107 us (27%)
  starting transfers between devices  87.7 us (22%)
  other arithmetic  11.9 us (3%)
    ppermute x84, waiting for transfers between devices, send(): return lax.ppermute(value, COL, self.shift(dz, dy, dc))  181 us
    ppermute x84, starting transfers between devices, send(): return lax.ppermute(value, COL, self.shift(dz, dy, dc))  87.7 us
    pallas_call x8, Pallas kernels, section_product(): pl.pallas_call(functools.partial(section_kernel, sec_idx, pair, subs), ou...  63.1 us
    pallas_call x3, Pallas kernels, features_of(): pl.pallas_call(functools.partial(feature_kernel, sections, sec), out_shap...  27.3 us
    pallas_call x2, Pallas kernels, older_product(): pl.pallas_call(functools.partial(older_kernel, pairs, subs, chunks), out_...  16.8 us
  transfers between devices with their start and end apart: 84, of which 31 were waited for; matrix products, arithmetic and copies ran while one was open for 3% of the time, Pallas kernels for 24%

profile of v2, /device:TPU:0, one launch (start us, length us, event | category | flops | bytes accessed | tf_op | source)
XLA Modules:
  0.0 391.7 jit_solution(17622984485016962639)
XLA Ops:
  0.6 7.5 %features.3 = (f32[256,128]{1,0:T(8,128)}, f32[256,128]{1,0:T(8,128)}) custom-call(s32[17]{0:T(128)} %stack.77.meta_ref, s32[2]{0:T(128)} %offsets_ref.5, s32[16384]{0:T(1024)} %ids_ref.5, f32[64,16384]{1,0:T(8,128)} %bitcast.22, f32[128,128]{1,0:T(8,128)} %bitcast.34, f32[64,1024]{1,0:T(8,128)} %bitcast.25), custom_call_target="tpu_custom_call" | custom-call | tf_op jit(solution)/shard_map/features/pallas_call | solution.py:265
  25.1 10.1 %collective-permute-done.20 = f32[1024,128]{1,0:T(8,128)S(1)} collective-permute-done((f32[1024,128]{1,0:T(8,128)S(1)}, f32[1024,128]{1,0:T(8,128)S(1)}, u32[]{:S(2)}, u32[]{:S(2)}) %collective-permute-start.20) | collective-permute-done | bytes 524320 | tf_op jit(solution)/shard_map/ppermute | solution.py:76
  40.1 6.0 %collective-permute-done.2 = f32[1024,128]{1,0:T(8,128)S(1)} collective-permute-done((f32[1024,128]{1,0:T(8,128)S(1)}, f32[1024,128]{1,0:T(8,128)S(1)}, u32[]{:S(2)}, u32[]{:S(2)}) %collective-permute-start.2) | collective-permute-done | bytes 524320 | tf_op jit(solution)/shard_map/ppermute | solution.py:76
  60.2 7.9 %collective-permute-done.25 = f32[256,128]{1,0:T(8,128)S(1)} collective-permute-done((f32[256,128]{1,0:T(8,128)S(1)}, f32[256,128]{1,0:T(8,128)S(1)}, u32[]{:S(2)}, u32[]{:S(2)}) %collective-permute-start.25) | collective-permute-done | bytes 131104 | tf_op jit(solution)/shard_map/ppermute | solution.py:76
  88.4 11.7 %collective-permute-done.9.refs_1_.refs_5_ = f32[1024,128]{1,0:T(8,128)S(1)} collective-permute-done((f32[1024,128]{1,0:T(8,128)S(1)}, f32[1024,128]{1,0:T(8,128)S(1)}, u32[]{:S(2)}, u32[]{:S(2)}) %collective-permute-start.9) | collective-permute-done | bytes 524320 | tf_op jit(solution)/shard_map/ppermute | solution.py:76
  100.1 7.7 %features.4 = (f32[256,128]{1,0:T(8,128)}, f32[256,128]{1,0:T(8,128)}) custom-call(s32[17]{0:T(128)} %stack.77.meta_ref, s32[2]{0:T(128)} %offsets_ref.5, s32[16384]{0:T(1024)} %ids_ref.5, f32[64,16384]{1,0:T(8,128)} %bitcast.23, f32[128,128]{1,0:T(8,128)} %bitcast.35, f32[64,1024]{1,0:T(8,128)} %bitcast.26), custom_call_target="tpu_custom_call" | custom-call | tf_op jit(solution)/shard_map/features/pallas_call | solution.py:265
  108.9 8.7 %shard_map.77 = (f32[1024,128]{1,0:T(8,128)}, f32[1024,128]{1,0:T(8,128)}, f32[1024,128]{1,0:T(8,128)}, f32[1024,128]{1,0:T(8,128)}) custom-call(s32[17]{0:T(128)} %stack.77.meta_ref, f32[4,4096,256]{2,1,0:T(8,128)} %diag_ref.15, f32[6,256,4096]{2,1,0:T(8,128)} %lower_ref.19, f32[256,128]{1,0:T(8,128)} %get-tuple-element.77.pending_ref, ...), custom_call_target="tpu_custom_call" | custom-call | tf_op jit(solution)/shard_map/pallas_call | solution.py:207
  118.1 8.9 %shard_map.74 = (f32[1024,128]{1,0:T(8,128)}, f32[1024,128]{1,0:T(8,128)}, f32[1024,128]{1,0:T(8,128)}, f32[1024,128]{1,0:T(8,128)}) custom-call(s32[17]{0:T(128)} %stack.77.meta_ref, f32[4,4096,256]{2,1,0:T(8,128)} %diag_ref.15, f32[6,256,4096]{2,1,0:T(8,128)} %lower_ref.19, f32[256,128]{1,0:T(8,128)} %get-tuple-element.56.pending_ref, ...), custom_call_target="tpu_custom_call" | custom-call | tf_op jit(solution)/shard_map/pallas_call | solution.py:207
  131.8 10.6 %collective-permute-done.44 = f32[1024,128]{1,0:T(8,128)S(1)} collective-permute-done((f32[1024,128]{1,0:T(8,128)S(1)}, f32[1024,128]{1,0:T(8,128)S(1)}, u32[]{:S(2)}, u32[]{:S(2)}) %collective-permute-start.44) | collective-permute-done | bytes 524320 | tf_op jit(solution)/shard_map/ppermute | solution.py:76
  147.0 5.9 %collective-permute-done.14 = f32[1024,128]{1,0:T(8,128)S(1)} collective-permute-done((f32[1024,128]{1,0:T(8,128)S(1)}, f32[1024,128]{1,0:T(8,128)S(1)}, u32[]{:S(2)}, u32[]{:S(2)}) %collective-permute-start.14) | collective-permute-done | bytes 524320 | tf_op jit(solution)/shard_map/ppermute | solution.py:76
  163.4 8.4 %collective-permute-done.49 = f32[256,128]{1,0:T(8,128)S(1)} collective-permute-done((f32[256,128]{1,0:T(8,128)S(1)}, f32[256,128]{1,0:T(8,128)S(1)}, u32[]{:S(2)}, u32[]{:S(2)}) %collective-permute-start.49) | collective-permute-done | bytes 131104 | tf_op jit(solution)/shard_map/ppermute | solution.py:76
  193.5 11.8 %collective-permute-done.33.refs_1_.refs_3_ = f32[1024,128]{1,0:T(8,128)S(1)} collective-permute-done((f32[1024,128]{1,0:T(8,128)S(1)}, f32[1024,128]{1,0:T(8,128)S(1)}, u32[]{:S(2)}, u32[]{:S(2)}) %collective-permute-start.33) | collective-permute-done | bytes 524320 | tf_op jit(solution)/shard_map/ppermute | solution.py:76
  205.3 12.1 %features.5 = (f32[256,128]{1,0:T(8,128)}, f32[256,128]{1,0:T(8,128)}, f32[256,128]{1,0:T(8,128)}, f32[256,128]{1,0:T(8,128)}) custom-call(s32[17]{0:T(128)} %stack.77.meta_ref, s32[2]{0:T(128)} %offsets_ref.5, s32[16384]{0:T(1024)} %ids_ref.5, f32[64,16384]{1,0:T(8,128)} %bitcast.24, f32[128,128]{1,0:T(8,128)} %bitcast.36, f32[64,1024]{1,0:T(8,128)} %bitcast.27), custom_call_target="tpu_custom_call" | custom-call | tf_op jit(solution)/shard_map/features/pallas_call | solution.py:265
  217.5 9.7 %older.2 = (f32[256,128]{1,0:T(8,128)}, f32[256,128]{1,0:T(8,128)}, f32[256,128]{1,0:T(8,128)}, f32[256,128]{1,0:T(8,128)}) custom-call(s32[17]{0:T(128)} %stack.77.meta_ref, f32[6,256,4096]{2,1,0:T(8,128)} %lower_ref.19, f32[256,128]{1,0:T(8,128)} %get-tuple-element.61.refs_0_, f32[256,128]{1,0:T(8,128)} %get-tuple-element.62.refs_1_, ...), custom_call_target="tpu_custom_call" | custom-call | tf_op jit(solution)/shard_map/older/pallas_call | solution.py:304
  228.2 8.7 %shard_map.79 = (f32[1024,128]{1,0:T(8,128)}, f32[1024,128]{1,0:T(8,128)}, f32[1024,128]{1,0:T(8,128)}, f32[1024,128]{1,0:T(8,128)}) custom-call(s32[17]{0:T(128)} %stack.77.meta_ref, f32[4,4096,256]{2,1,0:T(8,128)} %diag_ref.15, f32[6,256,4096]{2,1,0:T(8,128)} %lower_ref.19, f32[256,128]{1,0:T(8,128)} %get-tuple-element.87.pending_ref, ...), custom_call_target="tpu_custom_call" | custom-call | tf_op jit(solution)/shard_map/pallas_call | solution.py:207
  237.3 8.9 %shard_map.76 = (f32[1024,128]{1,0:T(8,128)}, f32[1024,128]{1,0:T(8,128)}, f32[1024,128]{1,0:T(8,128)}, f32[1024,128]{1,0:T(8,128)}) custom-call(s32[17]{0:T(128)} %stack.77.meta_ref, f32[4,4096,256]{2,1,0:T(8,128)} %diag_ref.15, f32[6,256,4096]{2,1,0:T(8,128)} %lower_ref.19, f32[256,128]{1,0:T(8,128)} %get-tuple-element.70.pending_ref, ...), custom_call_target="tpu_custom_call" | custom-call | tf_op jit(solution)/shard_map/pallas_call | solution.py:207
  251.0 10.7 %collective-permute-done.68 = f32[1024,128]{1,0:T(8,128)S(1)} collective-permute-done((f32[1024,128]{1,0:T(8,128)S(1)}, f32[1024,128]{1,0:T(8,128)S(1)}, u32[]{:S(2)}, u32[]{:S(2)}) %collective-permute-start.68) | collective-permute-done | bytes 524320 | tf_op jit(solution)/shard_map/ppermute | solution.py:76
  266.3 5.9 %collective-permute-done.38 = f32[1024,128]{1,0:T(8,128)S(1)} collective-permute-done((f32[1024,128]{1,0:T(8,128)S(1)}, f32[1024,128]{1,0:T(8,128)S(1)}, u32[]{:S(2)}, u32[]{:S(2)}) %collective-permute-start.38) | collective-permute-done | bytes 524320 | tf_op jit(solution)/shard_map/ppermute | solution.py:76
  283.0 7.5 %collective-permute-done.73 = f32[256,128]{1,0:T(8,128)S(1)} collective-permute-done((f32[256,128]{1,0:T(8,128)S(1)}, f32[256,128]{1,0:T(8,128)S(1)}, u32[]{:S(2)}, u32[]{:S(2)}) %collective-permute-start.73) | collective-permute-done | bytes 131104 | tf_op jit(solution)/shard_map/ppermute | solution.py:76
  312.7 11.8 %collective-permute-done.57.refs_1_ = f32[1024,128]{1,0:T(8,128)S(1)} collective-permute-done((f32[1024,128]{1,0:T(8,128)S(1)}, f32[1024,128]{1,0:T(8,128)S(1)}, u32[]{:S(2)}, u32[]{:S(2)}) %collective-permute-start.57) | collective-permute-done | bytes 524320 | tf_op jit(solution)/shard_map/ppermute | solution.py:76
  324.6 7.1 %older.3 = (f32[256,128]{1,0:T(8,128)}, f32[256,128]{1,0:T(8,128)}) custom-call(s32[17]{0:T(128)} %stack.77.meta_ref, f32[6,256,4096]{2,1,0:T(8,128)} %lower_ref.19, f32[256,128]{1,0:T(8,128)} %get-tuple-element.75.refs_0_, f32[256,128]{1,0:T(8,128)} %get-tuple-element.76.refs_1_, f32[1024,128]{1,0:T(8,128)} %copy-done.2, f32[1024,128]{1,0:T(8,128)} %copy-done.6, ...), custom_call_target="tpu_custom_call" | custom-call | tf_op jit(solution)/shard_map/older/pallas_call | solution.py:304
  331.7 8.7 %shard_map.80 = (f32[1024,128]{1,0:T(8,128)}, f32[1024,128]{1,0:T(8,128)}, f32[1024,128]{1,0:T(8,128)}, f32[1024,128]{1,0:T(8,128)}) custom-call(s32[17]{0:T(128)} %stack.77.meta_ref, f32[4,4096,256]{2,1,0:T(8,128)} %diag_ref.15, f32[6,256,4096]{2,1,0:T(8,128)} %lower_ref.19, f32[256,128]{1,0:T(8,128)} %get-tuple-element.92.pending_ref, ...), custom_call_target="tpu_custom_call" | custom-call | tf_op jit(solution)/shard_map/pallas_call | solution.py:207
  341.6 8.9 %shard_map.78 = (f32[1024,128]{1,0:T(8,128)}, f32[1024,128]{1,0:T(8,128)}, f32[1024,128]{1,0:T(8,128)}, f32[1024,128]{1,0:T(8,128)}) custom-call(s32[17]{0:T(128)} %stack.77.meta_ref, f32[4,4096,256]{2,1,0:T(8,128)} %diag_ref.15, f32[6,256,4096]{2,1,0:T(8,128)} %lower_ref.19, f32[256,128]{1,0:T(8,128)} %get-tuple-element.82.pending_ref, ...), custom_call_target="tpu_custom_call" | custom-call | tf_op jit(solution)/shard_map/pallas_call | solution.py:207
  355.3 10.7 %collective-permute-done.80 = f32[1024,128]{1,0:T(8,128)S(1)} collective-permute-done((f32[1024,128]{1,0:T(8,128)S(1)}, f32[1024,128]{1,0:T(8,128)S(1)}, u32[]{:S(2)}, u32[]{:S(2)}) %collective-permute-start.80) | collective-permute-done | bytes 524320 | tf_op jit(solution)/shard_map/ppermute | solution.py:76
  (251 shorter events, 175.1 us)
Async XLA Ops:
  22.4 17.7 %collective-permute-start = (f32[1024,128]{1,0:T(8,128)}, f32[1024,128]{1,0:T(8,128)S(1)}, u32[]{:S(2)}, u32[]{:S(2)}) collective-permute-start(f32[1024,128]{1,0:T(8,128)} %get-tuple-element.53), channel_id=1, source_target_pairs={{0,1},{1,0},{2,3},{3,2},{4,5},{5,4},{6,7},{7,6},{8,9},{9,8},{10,11... | collective-permute-start | bytes 1572872 | tf_op jit(solution)/shard_map/ppermute | solution.py:76
  23.6 22.5 %collective-permute-start.2 = (f32[1024,128]{1,0:T(8,128)S(1)}, f32[1024,128]{1,0:T(8,128)S(1)}, u32[]{:S(2)}, u32[]{:S(2)}) collective-permute-start(f32[1024,128]{1,0:T(8,128)S(1)} %add.176), channel_id=1, source_target_pairs={{0,2},{1,3},{2,0},{3,1},{4,6},{5,7},{6,4},{7,5},{8,10},{9,11},{10,... | collective-permute-start | bytes 1572872 | tf_op jit(solution)/shard_map/ppermute | solution.py:76
  68.1 19.7 %collective-permute-start.27 = (f32[1024,128]{1,0:T(8,128)S(1)}, f32[1024,128]{1,0:T(8,128)S(1)}, u32[]{:S(2)}, u32[]{:S(2)}) collective-permute-start(f32[1024,128]{1,0:T(8,128)S(1)} %pad_maximum_fusion.1.refs_8_.refs_0_), channel_id=1, source_target_pairs={{0,2},{1,3},{2,0},{3,1},{4,6},{5,7},{6,4},{7,5},{8,10},{9,11},{10,... | collective-permute-start | bytes 1572872 | tf_op jit(solution)/shard_map/ppermute | solution.py:76
  87.8 20.0 %collective-permute-start.28 = (f32[1024,128]{1,0:T(8,128)S(1)}, f32[1024,128]{1,0:T(8,128)S(1)}, u32[]{:S(2)}, u32[]{:S(2)}) collective-permute-start(f32[1024,128]{1,0:T(8,128)S(1)} %pad_maximum_fusion.1.refs_8_.refs_0_), channel_id=1, source_target_pairs={{0,1},{1,0},{2,3},{3,2},{4,5},{5,4},{6,7},{7,6},{8,9},{9,8},{10,11... | collective-permute-start | bytes 1572872 | tf_op jit(solution)/shard_map/ppermute | solution.py:76
  87.8 20.0 %collective-permute-start.29 = (f32[1024,128]{1,0:T(8,128)S(1)}, f32[1024,128]{1,0:T(8,128)S(1)}, u32[]{:S(2)}, u32[]{:S(2)}) collective-permute-start(f32[1024,128]{1,0:T(8,128)S(1)} %collective-permute-done.27.refs_9_.refs_1_), channel_id=1, source_target_pairs={{0,1},{1,0},{2,3},{3,2},{4,5},{5,4},{6,7},{7,6},{8,9},{9,8},{10,11... | collective-permute-start | bytes 1572872 | tf_op jit(solution)/shard_map/ppermute | solution.py:76
  88.3 29.7 %collective-permute-start.10 = (f32[1024,128]{1,0:T(8,128)S(1)}, f32[1024,128]{1,0:T(8,128)}, u32[]{:S(2)}, u32[]{:S(2)}) collective-permute-start(f32[1024,128]{1,0:T(8,128)S(1)} %pad_maximum_fusion.refs_0_.refs_4_), channel_id=1, source_target_pairs={{0,1},{1,0},{2,3},{3,2},{4,5},{5,4},{6,7},{7,6},{8,9},{9,8},{10,11... | collective-permute-start | bytes 1572872 | tf_op jit(solution)/shard_map/ppermute | solution.py:76
  100.1 17.9 %collective-permute-start.11 = (f32[1024,128]{1,0:T(8,128)S(1)}, f32[1024,128]{1,0:T(8,128)}, u32[]{:S(2)}, u32[]{:S(2)}) collective-permute-start(f32[1024,128]{1,0:T(8,128)S(1)} %collective-permute-done.9.refs_1_.refs_5_), channel_id=1, source_target_pairs={{0,1},{1,0},{2,3},{3,2},{4,5},{5,4},{6,7},{7,6},{8,9},{9,8},{10,11... | collective-permute-start | bytes 1572872 | tf_op jit(solution)/shard_map/ppermute | solution.py:76
  129.1 17.9 %collective-permute-start.12 = (f32[1024,128]{1,0:T(8,128)}, f32[1024,128]{1,0:T(8,128)S(1)}, u32[]{:S(2)}, u32[]{:S(2)}) collective-permute-start(f32[1024,128]{1,0:T(8,128)} %get-tuple-element.58), channel_id=1, source_target_pairs={{0,1},{1,0},{2,3},{3,2},{4,5},{5,4},{6,7},{7,6},{8,9},{9,8},{10,11... | collective-permute-start | bytes 1572872 | tf_op jit(solution)/shard_map/ppermute | solution.py:76
  130.2 22.6 %collective-permute-start.14 = (f32[1024,128]{1,0:T(8,128)S(1)}, f32[1024,128]{1,0:T(8,128)S(1)}, u32[]{:S(2)}, u32[]{:S(2)}) collective-permute-start(f32[1024,128]{1,0:T(8,128)S(1)} %add.182), channel_id=1, source_target_pairs={{0,2},{1,3},{2,0},{3,1},{4,6},{5,7},{6,4},{7,5},{8,10},{9,11},{10,... | collective-permute-start | bytes 1572872 | tf_op jit(solution)/shard_map/ppermute | solution.py:76
  161.0 17.4 %collective-permute-start.16 = (f32[256,128]{1,0:T(8,128)S(1)}, f32[256,128]{1,0:T(8,128)S(1)}, u32[]{:S(2)}, u32[]{:S(2)}) collective-permute-start(f32[256,128]{1,0:T(8,128)S(1)} %get-tuple-element.114), channel_id=1, source_target_pairs={{0,8},{1,9},{2,10},{3,11},{4,12},{5,13},{6,14},{7,15},{8,0},{9,1},... | collective-permute-start | bytes 393224 | tf_op jit(solution)/shard_map/ppermute | solution.py:76
  171.8 21.1 %collective-permute-start.51 = (f32[1024,128]{1,0:T(8,128)S(1)}, f32[1024,128]{1,0:T(8,128)S(1)}, u32[]{:S(2)}, u32[]{:S(2)}) collective-permute-start(f32[1024,128]{1,0:T(8,128)S(1)} %pad_maximum_fusion.3.refs_6_.refs_0_), channel_id=1, source_target_pairs={{0,2},{1,3},{2,0},{3,1},{4,6},{5,7},{6,4},{7,5},{8,10},{9,11},{10,... | collective-permute-start | bytes 1572872 | tf_op jit(solution)/shard_map/ppermute | solution.py:76
  192.9 34.2 %collective-permute-start.52 = (f32[1024,128]{1,0:T(8,128)S(1)}, f32[1024,128]{1,0:T(8,128)S(1)}, u32[]{:S(2)}, u32[]{:S(2)}) collective-permute-start(f32[1024,128]{1,0:T(8,128)S(1)} %pad_maximum_fusion.3.refs_6_.refs_0_), channel_id=1, source_target_pairs={{0,1},{1,0},{2,3},{3,2},{4,5},{5,4},{6,7},{7,6},{8,9},{9,8},{10,11... | collective-permute-start | bytes 1572872 | tf_op jit(solution)/shard_map/ppermute | solution.py:76
  192.9 34.3 %collective-permute-start.53 = (f32[1024,128]{1,0:T(8,128)S(1)}, f32[1024,128]{1,0:T(8,128)S(1)}, u32[]{:S(2)}, u32[]{:S(2)}) collective-permute-start(f32[1024,128]{1,0:T(8,128)S(1)} %collective-permute-done.51.refs_7_.refs_1_), channel_id=1, source_target_pairs={{0,1},{1,0},{2,3},{3,2},{4,5},{5,4},{6,7},{7,6},{8,9},{9,8},{10,11... | collective-permute-start | bytes 1572872 | tf_op jit(solution)/shard_map/ppermute | solution.py:76
  193.5 43.8 %collective-permute-start.34 = (f32[1024,128]{1,0:T(8,128)S(1)}, f32[1024,128]{1,0:T(8,128)}, u32[]{:S(2)}, u32[]{:S(2)}) collective-permute-start(f32[1024,128]{1,0:T(8,128)S(1)} %pad_maximum_fusion.2.refs_0_.refs_2_), channel_id=1, source_target_pairs={{0,1},{1,0},{2,3},{3,2},{4,5},{5,4},{6,7},{7,6},{8,9},{9,8},{10,11... | collective-permute-start | bytes 1572872 | tf_op jit(solution)/shard_map/ppermute | solution.py:76
  205.3 32.0 %collective-permute-start.35 = (f32[1024,128]{1,0:T(8,128)S(1)}, f32[1024,128]{1,0:T(8,128)}, u32[]{:S(2)}, u32[]{:S(2)}) collective-permute-start(f32[1024,128]{1,0:T(8,128)S(1)} %collective-permute-done.33.refs_1_.refs_3_), channel_id=1, source_target_pairs={{0,1},{1,0},{2,3},{3,2},{4,5},{5,4},{6,7},{7,6},{8,9},{9,8},{10,11... | collective-permute-start | bytes 1572872 | tf_op jit(solution)/shard_map/ppermute | solution.py:76
  248.4 17.9 %collective-permute-start.36 = (f32[1024,128]{1,0:T(8,128)}, f32[1024,128]{1,0:T(8,128)S(1)}, u32[]{:S(2)}, u32[]{:S(2)}) collective-permute-start(f32[1024,128]{1,0:T(8,128)} %get-tuple-element.72), channel_id=1, source_target_pairs={{0,1},{1,0},{2,3},{3,2},{4,5},{5,4},{6,7},{7,6},{8,9},{9,8},{10,11... | collective-permute-start | bytes 1572872 | tf_op jit(solution)/shard_map/ppermute | solution.py:76
  249.5 22.7 %collective-permute-start.38 = (f32[1024,128]{1,0:T(8,128)S(1)}, f32[1024,128]{1,0:T(8,128)S(1)}, u32[]{:S(2)}, u32[]{:S(2)}) collective-permute-start(f32[1024,128]{1,0:T(8,128)S(1)} %add.194), channel_id=1, source_target_pairs={{0,2},{1,3},{2,0},{3,1},{4,6},{5,7},{6,4},{7,5},{8,10},{9,11},{10,... | collective-permute-start | bytes 1572872 | tf_op jit(solution)/shard_map/ppermute | solution.py:76
  280.5 17.1 %collective-permute-start.40 = (f32[256,128]{1,0:T(8,128)S(1)}, f32[256,128]{1,0:T(8,128)S(1)}, u32[]{:S(2)}, u32[]{:S(2)}) collective-permute-start(f32[256,128]{1,0:T(8,128)S(1)} %get-tuple-element.102), channel_id=1, source_target_pairs={{0,8},{1,9},{2,10},{3,11},{4,12},{5,13},{6,14},{7,15},{8,0},{9,1},... | collective-permute-start | bytes 393224 | tf_op jit(solution)/shard_map/ppermute | solution.py:76
  290.6 21.5 %collective-permute-start.75 = (f32[1024,128]{1,0:T(8,128)S(1)}, f32[1024,128]{1,0:T(8,128)S(1)}, u32[]{:S(2)}, u32[]{:S(2)}) collective-permute-start(f32[1024,128]{1,0:T(8,128)S(1)} %pad_maximum_fusion.5.refs_0_), channel_id=1, source_target_pairs={{0,2},{1,3},{2,0},{3,1},{4,6},{5,7},{6,4},{7,5},{8,10},{9,11},{10,... | collective-permute-start | bytes 1572872 | tf_op jit(solution)/shard_map/ppermute | solution.py:76
  312.1 19.5 %collective-permute-start.76 = (f32[1024,128]{1,0:T(8,128)S(1)}, f32[1024,128]{1,0:T(8,128)}, u32[]{:S(2)}, u32[]{:S(2)}) collective-permute-start(f32[1024,128]{1,0:T(8,128)S(1)} %pad_maximum_fusion.5.refs_0_), channel_id=1, source_target_pairs={{0,1},{1,0},{2,3},{3,2},{4,5},{5,4},{6,7},{7,6},{8,9},{9,8},{10,11... | collective-permute-start | bytes 1572872 | tf_op jit(solution)/shard_map/ppermute | solution.py:76
  312.1 19.5 %collective-permute-start.77 = (f32[1024,128]{1,0:T(8,128)S(1)}, f32[1024,128]{1,0:T(8,128)}, u32[]{:S(2)}, u32[]{:S(2)}) collective-permute-start(f32[1024,128]{1,0:T(8,128)S(1)} %collective-permute-done.75.refs_1_), channel_id=1, source_target_pairs={{0,1},{1,0},{2,3},{3,2},{4,5},{5,4},{6,7},{7,6},{8,9},{9,8},{10,11... | collective-permute-start | bytes 1572872 | tf_op jit(solution)/shard_map/ppermute | solution.py:76
  312.7 28.2 %collective-permute-start.58 = (f32[1024,128]{1,0:T(8,128)S(1)}, f32[1024,128]{1,0:T(8,128)S(1)}, u32[]{:S(2)}, u32[]{:S(2)}) collective-permute-start(f32[1024,128]{1,0:T(8,128)S(1)} %pad_maximum_fusion.4.refs_0_), channel_id=1, source_target_pairs={{0,1},{1,0},{2,3},{3,2},{4,5},{5,4},{6,7},{7,6},{8,9},{9,8},{10,11... | collective-permute-start | bytes 1572872 | tf_op jit(solution)/shard_map/ppermute | solution.py:76
  352.6 19.0 %collective-permute-start.60 = (f32[1024,128]{1,0:T(8,128)}, f32[1024,128]{1,0:T(8,128)S(1)}, u32[]{:S(2)}, u32[]{:S(2)}) collective-permute-start(f32[1024,128]{1,0:T(8,128)} %get-tuple-element.84), channel_id=1, source_target_pairs={{0,1},{1,0},{2,3},{3,2},{4,5},{5,4},{6,7},{7,6},{8,9},{9,8},{10,11... | collective-permute-start | bytes 1572872 | tf_op jit(solution)/shard_map/ppermute | solution.py:76
  353.8 22.7 %collective-permute-start.62 = (f32[1024,128]{1,0:T(8,128)S(1)}, f32[1024,128]{1,0:T(8,128)S(1)}, u32[]{:S(2)}, u32[]{:S(2)}) collective-permute-start(f32[1024,128]{1,0:T(8,128)S(1)} %add.206), channel_id=1, source_target_pairs={{0,2},{1,3},{2,0},{3,1},{4,6},{5,7},{6,4},{7,5},{8,10},{9,11},{10,... | collective-permute-start | bytes 1572872 | tf_op jit(solution)/shard_map/ppermute | solution.py:76
  (87 other events, 1199.7 us)

commit v3 on v2

--- a/solution.py
+++ b/solution.py
@@ -118,13 +118,15 @@
                     w_copy(m, sub, k).start()
         l_copy(k).start()
 
-    def finish(total):
+    def finish(total, then=None):
         def step(k, carry):
             if stage != "lower":
                 for sub in range(subs):
                     for m in range(chunks):
                         w_copy(m, sub, k).wait()
             l_copy(k).wait()
+            if then is not None:
+                then(k)
             return carry - three_pass(lbuf[k], wbuf[k])
 
         return lax.fori_loop(0, outer, step, total)
@@ -154,12 +156,13 @@
         rows = pl.ds(pl.multiple_of(k * owned, owned), owned)
         return pltpu.make_async_copy(obuf.at[sub, rows, :], outs[sub].at[rows, :], osem.at[k * subs + sub])
 
-    for k in range(outer):
-        d_copy(k).start()
+    if finish is None:
+        for k in range(outer):
+            d_copy(k).start()
     x_copy.wait()
     x = xbuf[...]
     if finish is not None:
-        x = finish(x)
+        x = finish(x, lambda k: d_copy(k).start())
     width = x.shape[1]
     x_high, x_low = halves(x)
     both = jnp.concatenate([x_high, x_low], axis=1)
@@ -418,6 +421,7 @@
 
 
 STEPS = 6
+LAGS = lambda at: 0.5 if 0 < at < 5 else 1.5
 
 
 def step_order(nsec, chunks):
@@ -425,10 +429,10 @@
     for sec_idx in range(nsec):
         for step in range(STEPS if sec_idx + 1 < nsec else STEPS - 2):
             at = sec_idx * STEPS + step
-            lag = 0.5 if 0 < at < 5 else 1.5
+            lag = LAGS(at)
             keyed += [(at + m * lag, at, (m, sec_idx, step)) for m in range(chunks)]
         if sec_idx == 0:
-            for part, at in zip(range(len(feature_parts(nsec))), (3.6, 4.6)):
+            for part, at in zip(range(len(feature_parts(nsec))), (3.2, 4.6)):
                 keyed.append((at, at, (chunks, 0, part)))
         elif sec_idx < nsec - 1:
             at = sec_idx * STEPS + 1
@@ -437,7 +441,7 @@
 
 
 def feature_parts(nsec):
-    return [one for one in (list(range(1, min(2, nsec))), list(range(2, nsec))) if one]
+    return [one for one in (list(range(2, nsec)), list(range(1, min(2, nsec)))) if one]
 
 
 def solution(mesh):

time: 392 us -> 387 us (0.987)
  Pallas kernels: 107 us -> 102 us
    pallas_call x8, Pallas kernels: 63.1 us -> 57.7 us  [section_product(): pl.pallas_call(functools.partial(section_kernel, sec_idx, pair, subs), ou...]
  transfers between devices with their start and end apart: 84 -> 84, of which waited for: 31 -> 31; matrix products, arithmetic and copies ran while one was open for 3% -> 3% of each run, Pallas kernels for 24% -> 23%
where the time goes in v3:
time: 387 us; the launch traced here: 386 us
  waiting for transfers between devices  180 us (47%)
  Pallas kernels  102 us (26%)
  starting transfers between devices  88.2 us (23%)
  other arithmetic  11.9 us (3%)
    ppermute x84, waiting for transfers between devices, send(): return lax.ppermute(value, COL, self.shift(dz, dy, dc))  180 us
    ppermute x84, starting transfers between devices, send(): return lax.ppermute(value, COL, self.shift(dz, dy, dc))  88.2 us
    pallas_call x8, Pallas kernels, section_product(): pl.pallas_call(functools.partial(section_kernel, sec_idx, pair, subs), ou...  57.7 us
    pallas_call x3, Pallas kernels, features_of(): pl.pallas_call(functools.partial(feature_kernel, sections, sec), out_shap...  27.3 us
    pallas_call x2, Pallas kernels, older_product(): pl.pallas_call(functools.partial(older_kernel, pairs, subs, chunks), out_...  16.8 us
  transfers between devices with their start and end apart: 84, of which 31 were waited for; matrix products, arithmetic and copies ran while one was open for 3% of the time, Pallas kernels for 23%

profile of v3, /device:TPU:0, one launch (start us, length us, event | category | flops | bytes accessed | tf_op | source)
XLA Modules:
  0.0 386.2 jit_solution(6861253623473406154)
XLA Ops:
  0.6 7.5 %features.3 = (f32[256,128]{1,0:T(8,128)}, f32[256,128]{1,0:T(8,128)}) custom-call(s32[17]{0:T(128)} %stack.77.meta_ref, s32[2]{0:T(128)} %offsets_ref.5, s32[16384]{0:T(1024)} %ids_ref.5, f32[64,16384]{1,0:T(8,128)} %bitcast.22, f32[128,128]{1,0:T(8,128)} %bitcast.34, f32[64,1024]{1,0:T(8,128)} %bitcast.25), custom_call_target="tpu_custom_call" | custom-call | tf_op jit(solution)/shard_map/features/pallas_call | solution.py:268
  25.1 10.1 %collective-permute-done.20 = f32[1024,128]{1,0:T(8,128)S(1)} collective-permute-done((f32[1024,128]{1,0:T(8,128)S(1)}, f32[1024,128]{1,0:T(8,128)S(1)}, u32[]{:S(2)}, u32[]{:S(2)}) %collective-permute-start.20) | collective-permute-done | bytes 524320 | tf_op jit(solution)/shard_map/ppermute | solution.py:76
  40.1 6.0 %collective-permute-done.2 = f32[1024,128]{1,0:T(8,128)S(1)} collective-permute-done((f32[1024,128]{1,0:T(8,128)S(1)}, f32[1024,128]{1,0:T(8,128)S(1)}, u32[]{:S(2)}, u32[]{:S(2)}) %collective-permute-start.2) | collective-permute-done | bytes 524320 | tf_op jit(solution)/shard_map/ppermute | solution.py:76
  60.2 7.9 %collective-permute-done.25 = f32[256,128]{1,0:T(8,128)S(1)} collective-permute-done((f32[256,128]{1,0:T(8,128)S(1)}, f32[256,128]{1,0:T(8,128)S(1)}, u32[]{:S(2)}, u32[]{:S(2)}) %collective-permute-start.25) | collective-permute-done | bytes 131104 | tf_op jit(solution)/shard_map/ppermute | solution.py:76
  88.4 11.7 %collective-permute-done.9.refs_1_.refs_5_ = f32[1024,128]{1,0:T(8,128)S(1)} collective-permute-done((f32[1024,128]{1,0:T(8,128)S(1)}, f32[1024,128]{1,0:T(8,128)S(1)}, u32[]{:S(2)}, u32[]{:S(2)}) %collective-permute-start.9) | collective-permute-done | bytes 524320 | tf_op jit(solution)/shard_map/ppermute | solution.py:76
  100.1 7.7 %features.4 = (f32[256,128]{1,0:T(8,128)}, f32[256,128]{1,0:T(8,128)}) custom-call(s32[17]{0:T(128)} %stack.77.meta_ref, s32[2]{0:T(128)} %offsets_ref.5, s32[16384]{0:T(1024)} %ids_ref.5, f32[64,16384]{1,0:T(8,128)} %bitcast.23, f32[128,128]{1,0:T(8,128)} %bitcast.35, f32[64,1024]{1,0:T(8,128)} %bitcast.26), custom_call_target="tpu_custom_call" | custom-call | tf_op jit(solution)/shard_map/features/pallas_call | solution.py:268
  108.9 7.8 %shard_map.77 = (f32[1024,128]{1,0:T(8,128)}, f32[1024,128]{1,0:T(8,128)}, f32[1024,128]{1,0:T(8,128)}, f32[1024,128]{1,0:T(8,128)}) custom-call(s32[17]{0:T(128)} %stack.77.meta_ref, f32[4,4096,256]{2,1,0:T(8,128)} %diag_ref.15, f32[6,256,4096]{2,1,0:T(8,128)} %lower_ref.19, f32[256,128]{1,0:T(8,128)} %get-tuple-element.77.pending_ref, ...), custom_call_target="tpu_custom_call" | custom-call | tf_op jit(solution)/shard_map/pallas_call | solution.py:210
  117.2 8.0 %shard_map.74 = (f32[1024,128]{1,0:T(8,128)}, f32[1024,128]{1,0:T(8,128)}, f32[1024,128]{1,0:T(8,128)}, f32[1024,128]{1,0:T(8,128)}) custom-call(s32[17]{0:T(128)} %stack.77.meta_ref, f32[4,4096,256]{2,1,0:T(8,128)} %diag_ref.15, f32[6,256,4096]{2,1,0:T(8,128)} %lower_ref.19, f32[256,128]{1,0:T(8,128)} %get-tuple-element.56.pending_ref, ...), custom_call_target="tpu_custom_call" | custom-call | tf_op jit(solution)/shard_map/pallas_call | solution.py:210
  130.0 10.6 %collective-permute-done.44 = f32[1024,128]{1,0:T(8,128)S(1)} collective-permute-done((f32[1024,128]{1,0:T(8,128)S(1)}, f32[1024,128]{1,0:T(8,128)S(1)}, u32[]{:S(2)}, u32[]{:S(2)}) %collective-permute-start.44) | collective-permute-done | bytes 524320 | tf_op jit(solution)/shard_map/ppermute | solution.py:76
  145.2 5.9 %collective-permute-done.14 = f32[1024,128]{1,0:T(8,128)S(1)} collective-permute-done((f32[1024,128]{1,0:T(8,128)S(1)}, f32[1024,128]{1,0:T(8,128)S(1)}, u32[]{:S(2)}, u32[]{:S(2)}) %collective-permute-start.14) | collective-permute-done | bytes 524320 | tf_op jit(solution)/shard_map/ppermute | solution.py:76
  161.6 8.3 %collective-permute-done.49 = f32[256,128]{1,0:T(8,128)S(1)} collective-permute-done((f32[256,128]{1,0:T(8,128)S(1)}, f32[256,128]{1,0:T(8,128)S(1)}, u32[]{:S(2)}, u32[]{:S(2)}) %collective-permute-start.49) | collective-permute-done | bytes 131104 | tf_op jit(solution)/shard_map/ppermute | solution.py:76
  191.8 11.7 %collective-permute-done.33.refs_1_.refs_3_ = f32[1024,128]{1,0:T(8,128)S(1)} collective-permute-done((f32[1024,128]{1,0:T(8,128)S(1)}, f32[1024,128]{1,0:T(8,128)S(1)}, u32[]{:S(2)}, u32[]{:S(2)}) %collective-permute-start.33) | collective-permute-done | bytes 524320 | tf_op jit(solution)/shard_map/ppermute | solution.py:76
  203.5 12.1 %features.5 = (f32[256,128]{1,0:T(8,128)}, f32[256,128]{1,0:T(8,128)}, f32[256,128]{1,0:T(8,128)}, f32[256,128]{1,0:T(8,128)}) custom-call(s32[17]{0:T(128)} %stack.77.meta_ref, s32[2]{0:T(128)} %offsets_ref.5, s32[16384]{0:T(1024)} %ids_ref.5, f32[64,16384]{1,0:T(8,128)} %bitcast.24, f32[128,128]{1,0:T(8,128)} %bitcast.36, f32[64,1024]{1,0:T(8,128)} %bitcast.27), custom_call_target="tpu_custom_call" | custom-call | tf_op jit(solution)/shard_map/features/pallas_call | solution.py:268
  215.7 9.7 %older.2 = (f32[256,128]{1,0:T(8,128)}, f32[256,128]{1,0:T(8,128)}, f32[256,128]{1,0:T(8,128)}, f32[256,128]{1,0:T(8,128)}) custom-call(s32[17]{0:T(128)} %stack.77.meta_ref, f32[6,256,4096]{2,1,0:T(8,128)} %lower_ref.19, f32[256,128]{1,0:T(8,128)} %get-tuple-element.61.refs_0_, f32[256,128]{1,0:T(8,128)} %get-tuple-element.62.refs_1_, ...), custom_call_target="tpu_custom_call" | custom-call | tf_op jit(solution)/shard_map/older/pallas_call | solution.py:307
  226.4 7.8 %shard_map.79 = (f32[1024,128]{1,0:T(8,128)}, f32[1024,128]{1,0:T(8,128)}, f32[1024,128]{1,0:T(8,128)}, f32[1024,128]{1,0:T(8,128)}) custom-call(s32[17]{0:T(128)} %stack.77.meta_ref, f32[4,4096,256]{2,1,0:T(8,128)} %diag_ref.15, f32[6,256,4096]{2,1,0:T(8,128)} %lower_ref.19, f32[256,128]{1,0:T(8,128)} %get-tuple-element.87.pending_ref, ...), custom_call_target="tpu_custom_call" | custom-call | tf_op jit(solution)/shard_map/pallas_call | solution.py:210
  234.6 8.0 %shard_map.76 = (f32[1024,128]{1,0:T(8,128)}, f32[1024,128]{1,0:T(8,128)}, f32[1024,128]{1,0:T(8,128)}, f32[1024,128]{1,0:T(8,128)}) custom-call(s32[17]{0:T(128)} %stack.77.meta_ref, f32[4,4096,256]{2,1,0:T(8,128)} %diag_ref.15, f32[6,256,4096]{2,1,0:T(8,128)} %lower_ref.19, f32[256,128]{1,0:T(8,128)} %get-tuple-element.70.pending_ref, ...), custom_call_target="tpu_custom_call" | custom-call | tf_op jit(solution)/shard_map/pallas_call | solution.py:210
  247.4 10.6 %collective-permute-done.68 = f32[1024,128]{1,0:T(8,128)S(1)} collective-permute-done((f32[1024,128]{1,0:T(8,128)S(1)}, f32[1024,128]{1,0:T(8,128)S(1)}, u32[]{:S(2)}, u32[]{:S(2)}) %collective-permute-start.68) | collective-permute-done | bytes 524320 | tf_op jit(solution)/shard_map/ppermute | solution.py:76
  262.7 5.9 %collective-permute-done.38 = f32[1024,128]{1,0:T(8,128)S(1)} collective-permute-done((f32[1024,128]{1,0:T(8,128)S(1)}, f32[1024,128]{1,0:T(8,128)S(1)}, u32[]{:S(2)}, u32[]{:S(2)}) %collective-permute-start.38) | collective-permute-done | bytes 524320 | tf_op jit(solution)/shard_map/ppermute | solution.py:76
  279.4 7.6 %collective-permute-done.73 = f32[256,128]{1,0:T(8,128)S(1)} collective-permute-done((f32[256,128]{1,0:T(8,128)S(1)}, f32[256,128]{1,0:T(8,128)S(1)}, u32[]{:S(2)}, u32[]{:S(2)}) %collective-permute-start.73) | collective-permute-done | bytes 131104 | tf_op jit(solution)/shard_map/ppermute | solution.py:76
  309.2 11.8 %collective-permute-done.57.refs_1_ = f32[1024,128]{1,0:T(8,128)S(1)} collective-permute-done((f32[1024,128]{1,0:T(8,128)S(1)}, f32[1024,128]{1,0:T(8,128)S(1)}, u32[]{:S(2)}, u32[]{:S(2)}) %collective-permute-start.57) | collective-permute-done | bytes 524320 | tf_op jit(solution)/shard_map/ppermute | solution.py:76
  320.9 7.1 %older.3 = (f32[256,128]{1,0:T(8,128)}, f32[256,128]{1,0:T(8,128)}) custom-call(s32[17]{0:T(128)} %stack.77.meta_ref, f32[6,256,4096]{2,1,0:T(8,128)} %lower_ref.19, f32[256,128]{1,0:T(8,128)} %get-tuple-element.75.refs_0_, f32[256,128]{1,0:T(8,128)} %get-tuple-element.76.refs_1_, f32[1024,128]{1,0:T(8,128)} %copy-done.2, f32[1024,128]{1,0:T(8,128)} %copy-done.6, ...), custom_call_target="tpu_custom_call" | custom-call | tf_op jit(solution)/shard_map/older/pallas_call | solution.py:307
  328.1 7.8 %shard_map.80 = (f32[1024,128]{1,0:T(8,128)}, f32[1024,128]{1,0:T(8,128)}, f32[1024,128]{1,0:T(8,128)}, f32[1024,128]{1,0:T(8,128)}) custom-call(s32[17]{0:T(128)} %stack.77.meta_ref, f32[4,4096,256]{2,1,0:T(8,128)} %diag_ref.15, f32[6,256,4096]{2,1,0:T(8,128)} %lower_ref.19, f32[256,128]{1,0:T(8,128)} %get-tuple-element.92.pending_ref, ...), custom_call_target="tpu_custom_call" | custom-call | tf_op jit(solution)/shard_map/pallas_call | solution.py:210
  337.1 8.0 %shard_map.78 = (f32[1024,128]{1,0:T(8,128)}, f32[1024,128]{1,0:T(8,128)}, f32[1024,128]{1,0:T(8,128)}, f32[1024,128]{1,0:T(8,128)}) custom-call(s32[17]{0:T(128)} %stack.77.meta_ref, f32[4,4096,256]{2,1,0:T(8,128)} %diag_ref.15, f32[6,256,4096]{2,1,0:T(8,128)} %lower_ref.19, f32[256,128]{1,0:T(8,128)} %get-tuple-element.82.pending_ref, ...), custom_call_target="tpu_custom_call" | custom-call | tf_op jit(solution)/shard_map/pallas_call | solution.py:210
  349.9 10.7 %collective-permute-done.80 = f32[1024,128]{1,0:T(8,128)S(1)} collective-permute-done((f32[1024,128]{1,0:T(8,128)S(1)}, f32[1024,128]{1,0:T(8,128)S(1)}, u32[]{:S(2)}, u32[]{:S(2)}) %collective-permute-start.80) | collective-permute-done | bytes 524320 | tf_op jit(solution)/shard_map/ppermute | solution.py:76
  (251 shorter events, 175.4 us)
Async XLA Ops:
  22.4 17.7 %collective-permute-start = (f32[1024,128]{1,0:T(8,128)}, f32[1024,128]{1,0:T(8,128)S(1)}, u32[]{:S(2)}, u32[]{:S(2)}) collective-permute-start(f32[1024,128]{1,0:T(8,128)} %get-tuple-element.53), channel_id=1, source_target_pairs={{0,1},{1,0},{2,3},{3,2},{4,5},{5,4},{6,7},{7,6},{8,9},{9,8},{10,11... | collective-permute-start | bytes 1572872 | tf_op jit(solution)/shard_map/ppermute | solution.py:76
  23.6 22.5 %collective-permute-start.2 = (f32[1024,128]{1,0:T(8,128)S(1)}, f32[1024,128]{1,0:T(8,128)S(1)}, u32[]{:S(2)}, u32[]{:S(2)}) collective-permute-start(f32[1024,128]{1,0:T(8,128)S(1)} %add.176), channel_id=1, source_target_pairs={{0,2},{1,3},{2,0},{3,1},{4,6},{5,7},{6,4},{7,5},{8,10},{9,11},{10,... | collective-permute-start | bytes 1572872 | tf_op jit(solution)/shard_map/ppermute | solution.py:76
  68.1 19.7 %collective-permute-start.27 = (f32[1024,128]{1,0:T(8,128)S(1)}, f32[1024,128]{1,0:T(8,128)S(1)}, u32[]{:S(2)}, u32[]{:S(2)}) collective-permute-start(f32[1024,128]{1,0:T(8,128)S(1)} %pad_maximum_fusion.1.refs_8_.refs_0_), channel_id=1, source_target_pairs={{0,2},{1,3},{2,0},{3,1},{4,6},{5,7},{6,4},{7,5},{8,10},{9,11},{10,... | collective-permute-start | bytes 1572872 | tf_op jit(solution)/shard_map/ppermute | solution.py:76
  87.8 20.0 %collective-permute-start.28 = (f32[1024,128]{1,0:T(8,128)S(1)}, f32[1024,128]{1,0:T(8,128)S(1)}, u32[]{:S(2)}, u32[]{:S(2)}) collective-permute-start(f32[1024,128]{1,0:T(8,128)S(1)} %pad_maximum_fusion.1.refs_8_.refs_0_), channel_id=1, source_target_pairs={{0,1},{1,0},{2,3},{3,2},{4,5},{5,4},{6,7},{7,6},{8,9},{9,8},{10,11... | collective-permute-start | bytes 1572872 | tf_op jit(solution)/shard_map/ppermute | solution.py:76
  87.8 20.0 %collective-permute-start.29 = (f32[1024,128]{1,0:T(8,128)S(1)}, f32[1024,128]{1,0:T(8,128)S(1)}, u32[]{:S(2)}, u32[]{:S(2)}) collective-permute-start(f32[1024,128]{1,0:T(8,128)S(1)} %collective-permute-done.27.refs_9_.refs_1_), channel_id=1, source_target_pairs={{0,1},{1,0},{2,3},{3,2},{4,5},{5,4},{6,7},{7,6},{8,9},{9,8},{10,11... | collective-permute-start | bytes 1572872 | tf_op jit(solution)/shard_map/ppermute | solution.py:76
  88.3 28.8 %collective-permute-start.10 = (f32[1024,128]{1,0:T(8,128)S(1)}, f32[1024,128]{1,0:T(8,128)}, u32[]{:S(2)}, u32[]{:S(2)}) collective-permute-start(f32[1024,128]{1,0:T(8,128)S(1)} %pad_maximum_fusion.refs_0_.refs_4_), channel_id=1, source_target_pairs={{0,1},{1,0},{2,3},{3,2},{4,5},{5,4},{6,7},{7,6},{8,9},{9,8},{10,11... | collective-permute-start | bytes 1572872 | tf_op jit(solution)/shard_map/ppermute | solution.py:76
  100.1 17.0 %collective-permute-start.11 = (f32[1024,128]{1,0:T(8,128)S(1)}, f32[1024,128]{1,0:T(8,128)}, u32[]{:S(2)}, u32[]{:S(2)}) collective-permute-start(f32[1024,128]{1,0:T(8,128)S(1)} %collective-permute-done.9.refs_1_.refs_5_), channel_id=1, source_target_pairs={{0,1},{1,0},{2,3},{3,2},{4,5},{5,4},{6,7},{7,6},{8,9},{9,8},{10,11... | collective-permute-start | bytes 1572872 | tf_op jit(solution)/shard_map/ppermute | solution.py:76
  127.3 17.9 %collective-permute-start.12 = (f32[1024,128]{1,0:T(8,128)}, f32[1024,128]{1,0:T(8,128)S(1)}, u32[]{:S(2)}, u32[]{:S(2)}) collective-permute-start(f32[1024,128]{1,0:T(8,128)} %get-tuple-element.58), channel_id=1, source_target_pairs={{0,1},{1,0},{2,3},{3,2},{4,5},{5,4},{6,7},{7,6},{8,9},{9,8},{10,11... | collective-permute-start | bytes 1572872 | tf_op jit(solution)/shard_map/ppermute | solution.py:76
  128.4 22.6 %collective-permute-start.14 = (f32[1024,128]{1,0:T(8,128)S(1)}, f32[1024,128]{1,0:T(8,128)S(1)}, u32[]{:S(2)}, u32[]{:S(2)}) collective-permute-start(f32[1024,128]{1,0:T(8,128)S(1)} %add.182), channel_id=1, source_target_pairs={{0,2},{1,3},{2,0},{3,1},{4,6},{5,7},{6,4},{7,5},{8,10},{9,11},{10,... | collective-permute-start | bytes 1572872 | tf_op jit(solution)/shard_map/ppermute | solution.py:76
  159.2 17.4 %collective-permute-start.16 = (f32[256,128]{1,0:T(8,128)S(1)}, f32[256,128]{1,0:T(8,128)S(1)}, u32[]{:S(2)}, u32[]{:S(2)}) collective-permute-start(f32[256,128]{1,0:T(8,128)S(1)} %get-tuple-element.114), channel_id=1, source_target_pairs={{0,8},{1,9},{2,10},{3,11},{4,12},{5,13},{6,14},{7,15},{8,0},{9,1},... | collective-permute-start | bytes 393224 | tf_op jit(solution)/shard_map/ppermute | solution.py:76
  170.0 21.2 %collective-permute-start.51 = (f32[1024,128]{1,0:T(8,128)S(1)}, f32[1024,128]{1,0:T(8,128)S(1)}, u32[]{:S(2)}, u32[]{:S(2)}) collective-permute-start(f32[1024,128]{1,0:T(8,128)S(1)} %pad_maximum_fusion.3.refs_6_.refs_0_), channel_id=1, source_target_pairs={{0,2},{1,3},{2,0},{3,1},{4,6},{5,7},{6,4},{7,5},{8,10},{9,11},{10,... | collective-permute-start | bytes 1572872 | tf_op jit(solution)/shard_map/ppermute | solution.py:76
  191.2 34.2 %collective-permute-start.52 = (f32[1024,128]{1,0:T(8,128)S(1)}, f32[1024,128]{1,0:T(8,128)S(1)}, u32[]{:S(2)}, u32[]{:S(2)}) collective-permute-start(f32[1024,128]{1,0:T(8,128)S(1)} %pad_maximum_fusion.3.refs_6_.refs_0_), channel_id=1, source_target_pairs={{0,1},{1,0},{2,3},{3,2},{4,5},{5,4},{6,7},{7,6},{8,9},{9,8},{10,11... | collective-permute-start | bytes 1572872 | tf_op jit(solution)/shard_map/ppermute | solution.py:76
  191.2 34.2 %collective-permute-start.53 = (f32[1024,128]{1,0:T(8,128)S(1)}, f32[1024,128]{1,0:T(8,128)S(1)}, u32[]{:S(2)}, u32[]{:S(2)}) collective-permute-start(f32[1024,128]{1,0:T(8,128)S(1)} %collective-permute-done.51.refs_7_.refs_1_), channel_id=1, source_target_pairs={{0,1},{1,0},{2,3},{3,2},{4,5},{5,4},{6,7},{7,6},{8,9},{9,8},{10,11... | collective-permute-start | bytes 1572872 | tf_op jit(solution)/shard_map/ppermute | solution.py:76
  191.7 42.9 %collective-permute-start.34 = (f32[1024,128]{1,0:T(8,128)S(1)}, f32[1024,128]{1,0:T(8,128)}, u32[]{:S(2)}, u32[]{:S(2)}) collective-permute-start(f32[1024,128]{1,0:T(8,128)S(1)} %pad_maximum_fusion.2.refs_0_.refs_2_), channel_id=1, source_target_pairs={{0,1},{1,0},{2,3},{3,2},{4,5},{5,4},{6,7},{7,6},{8,9},{9,8},{10,11... | collective-permute-start | bytes 1572872 | tf_op jit(solution)/shard_map/ppermute | solution.py:76
  203.5 31.1 %collective-permute-start.35 = (f32[1024,128]{1,0:T(8,128)S(1)}, f32[1024,128]{1,0:T(8,128)}, u32[]{:S(2)}, u32[]{:S(2)}) collective-permute-start(f32[1024,128]{1,0:T(8,128)S(1)} %collective-permute-done.33.refs_1_.refs_3_), channel_id=1, source_target_pairs={{0,1},{1,0},{2,3},{3,2},{4,5},{5,4},{6,7},{7,6},{8,9},{9,8},{10,11... | collective-permute-start | bytes 1572872 | tf_op jit(solution)/shard_map/ppermute | solution.py:76
  244.8 17.9 %collective-permute-start.36 = (f32[1024,128]{1,0:T(8,128)}, f32[1024,128]{1,0:T(8,128)S(1)}, u32[]{:S(2)}, u32[]{:S(2)}) collective-permute-start(f32[1024,128]{1,0:T(8,128)} %get-tuple-element.72), channel_id=1, source_target_pairs={{0,1},{1,0},{2,3},{3,2},{4,5},{5,4},{6,7},{7,6},{8,9},{9,8},{10,11... | collective-permute-start | bytes 1572872 | tf_op jit(solution)/shard_map/ppermute | solution.py:76
  245.9 22.6 %collective-permute-start.38 = (f32[1024,128]{1,0:T(8,128)S(1)}, f32[1024,128]{1,0:T(8,128)S(1)}, u32[]{:S(2)}, u32[]{:S(2)}) collective-permute-start(f32[1024,128]{1,0:T(8,128)S(1)} %add.194), channel_id=1, source_target_pairs={{0,2},{1,3},{2,0},{3,1},{4,6},{5,7},{6,4},{7,5},{8,10},{9,11},{10,... | collective-permute-start | bytes 1572872 | tf_op jit(solution)/shard_map/ppermute | solution.py:76
  276.9 17.1 %collective-permute-start.40 = (f32[256,128]{1,0:T(8,128)S(1)}, f32[256,128]{1,0:T(8,128)S(1)}, u32[]{:S(2)}, u32[]{:S(2)}) collective-permute-start(f32[256,128]{1,0:T(8,128)S(1)} %get-tuple-element.102), channel_id=1, source_target_pairs={{0,8},{1,9},{2,10},{3,11},{4,12},{5,13},{6,14},{7,15},{8,0},{9,1},... | collective-permute-start | bytes 393224 | tf_op jit(solution)/shard_map/ppermute | solution.py:76
  287.0 21.6 %collective-permute-start.75 = (f32[1024,128]{1,0:T(8,128)S(1)}, f32[1024,128]{1,0:T(8,128)S(1)}, u32[]{:S(2)}, u32[]{:S(2)}) collective-permute-start(f32[1024,128]{1,0:T(8,128)S(1)} %pad_maximum_fusion.5.refs_0_), channel_id=1, source_target_pairs={{0,2},{1,3},{2,0},{3,1},{4,6},{5,7},{6,4},{7,5},{8,10},{9,11},{10,... | collective-permute-start | bytes 1572872 | tf_op jit(solution)/shard_map/ppermute | solution.py:76
  308.6 19.5 %collective-permute-start.76 = (f32[1024,128]{1,0:T(8,128)S(1)}, f32[1024,128]{1,0:T(8,128)}, u32[]{:S(2)}, u32[]{:S(2)}) collective-permute-start(f32[1024,128]{1,0:T(8,128)S(1)} %pad_maximum_fusion.5.refs_0_), channel_id=1, source_target_pairs={{0,1},{1,0},{2,3},{3,2},{4,5},{5,4},{6,7},{7,6},{8,9},{9,8},{10,11... | collective-permute-start | bytes 1572872 | tf_op jit(solution)/shard_map/ppermute | solution.py:76
  308.6 19.5 %collective-permute-start.77 = (f32[1024,128]{1,0:T(8,128)S(1)}, f32[1024,128]{1,0:T(8,128)}, u32[]{:S(2)}, u32[]{:S(2)}) collective-permute-start(f32[1024,128]{1,0:T(8,128)S(1)} %collective-permute-done.75.refs_1_), channel_id=1, source_target_pairs={{0,1},{1,0},{2,3},{3,2},{4,5},{5,4},{6,7},{7,6},{8,9},{9,8},{10,11... | collective-permute-start | bytes 1572872 | tf_op jit(solution)/shard_map/ppermute | solution.py:76
  309.1 27.2 %collective-permute-start.58 = (f32[1024,128]{1,0:T(8,128)S(1)}, f32[1024,128]{1,0:T(8,128)S(1)}, u32[]{:S(2)}, u32[]{:S(2)}) collective-permute-start(f32[1024,128]{1,0:T(8,128)S(1)} %pad_maximum_fusion.4.refs_0_), channel_id=1, source_target_pairs={{0,1},{1,0},{2,3},{3,2},{4,5},{5,4},{6,7},{7,6},{8,9},{9,8},{10,11... | collective-permute-start | bytes 1572872 | tf_op jit(solution)/shard_map/ppermute | solution.py:76
  347.3 18.9 %collective-permute-start.60 = (f32[1024,128]{1,0:T(8,128)}, f32[1024,128]{1,0:T(8,128)S(1)}, u32[]{:S(2)}, u32[]{:S(2)}) collective-permute-start(f32[1024,128]{1,0:T(8,128)} %get-tuple-element.84), channel_id=1, source_target_pairs={{0,1},{1,0},{2,3},{3,2},{4,5},{5,4},{6,7},{7,6},{8,9},{9,8},{10,11... | collective-permute-start | bytes 1572872 | tf_op jit(solution)/shard_map/ppermute | solution.py:76
  348.4 22.7 %collective-permute-start.62 = (f32[1024,128]{1,0:T(8,128)S(1)}, f32[1024,128]{1,0:T(8,128)S(1)}, u32[]{:S(2)}, u32[]{:S(2)}) collective-permute-start(f32[1024,128]{1,0:T(8,128)S(1)} %add.206), channel_id=1, source_target_pairs={{0,2},{1,3},{2,0},{3,1},{4,6},{5,7},{6,4},{7,5},{8,10},{9,11},{10,... | collective-permute-start | bytes 1572872 | tf_op jit(solution)/shard_map/ppermute | solution.py:76
  (87 other events, 1187.3 us)

commit v4 on v3

--- a/solution.py
+++ b/solution.py
@@ -248,7 +248,7 @@
                 return centers, rates
 
             zero = jnp.zeros((features, lanes), jnp.float32)
-            centers, rates = lax.fori_loop(0, lanes, pick, (zero, zero[:1]), unroll=16)
+            centers, rates = lax.fori_loop(0, lanes, pick, (zero, zero[:1]), unroll=32)
             pad = lanes - features
             flat = jnp.concatenate([centers, jnp.broadcast_to(rates, (pad, lanes))], axis=0).T
             centers, rates = flat[:, :features], flat[:, features : features + 1]
@@ -421,6 +421,7 @@
 
 
 STEPS = 6
+FOUND = "001101021020100110101201010011010101201010110101"
 LAGS = lambda at: 0.5 if 0 < at < 5 else 1.5
 
 
@@ -437,7 +438,12 @@
         elif sec_idx < nsec - 1:
             at = sec_idx * STEPS + 1
             keyed.append((at + 1.5 * (chunks - 1), at + 1, (chunks, sec_idx, 0)))
-    return [entry for _, _, entry in sorted(keyed)]
+    order = [entry for _, _, entry in sorted(keyed)]
+    streams = [iter(sorted(entry[1:] for entry in order if entry[0] == m)) for m in range(chunks + 1)]
+    found = [int(one) for one in FOUND]
+    if sorted(found) == sorted(entry[0] for entry in order):
+        order = [(m, *next(streams[m])) for m in found]
+    return order
 
 
 def feature_parts(nsec):

time: 387 us -> 385 us (level)
  no operation moved by 1% of the time
where the time goes in v4:
time: 385 us; the launch traced here: 384 us
  waiting for transfers between devices  180 us (47%)
  Pallas kernels  99.8 us (26%)
  starting transfers between devices  88.2 us (23%)
  other arithmetic  11.9 us (3%)
    ppermute x84, waiting for transfers between devices, send(): return lax.ppermute(value, COL, self.shift(dz, dy, dc))  180 us
    ppermute x84, starting transfers between devices, send(): return lax.ppermute(value, COL, self.shift(dz, dy, dc))  88.2 us
    pallas_call x8, Pallas kernels, section_product(): pl.pallas_call(functools.partial(section_kernel, sec_idx, pair, subs), ou...  57.7 us
    pallas_call x3, Pallas kernels, features_of(): pl.pallas_call(functools.partial(feature_kernel, sections, sec), out_shap...  25.3 us
    pallas_call x2, Pallas kernels, older_product(): pl.pallas_call(functools.partial(older_kernel, pairs, subs, chunks), out_...  16.7 us
  transfers between devices with their start and end apart: 84, of which 31 were waited for; matrix products, arithmetic and copies ran while one was open for 3% of the time, Pallas kernels for 23%

profile of v4, /device:TPU:0, one launch (start us, length us, event | category | flops | bytes accessed | tf_op | source)
XLA Modules:
  0.0 384.2 jit_solution(3217894299683186567)
XLA Ops:
  0.6 7.0 %features.3 = (f32[256,128]{1,0:T(8,128)}, f32[256,128]{1,0:T(8,128)}) custom-call(s32[17]{0:T(128)} %stack.77.meta_ref, s32[2]{0:T(128)} %offsets_ref.5, s32[16384]{0:T(1024)} %ids_ref.5, f32[64,16384]{1,0:T(8,128)} %bitcast.22, f32[128,128]{1,0:T(8,128)} %bitcast.34, f32[64,1024]{1,0:T(8,128)} %bitcast.25), custom_call_target="tpu_custom_call" | custom-call | tf_op jit(solution)/shard_map/features/pallas_call | solution.py:268
  24.6 10.1 %collective-permute-done.20 = f32[1024,128]{1,0:T(8,128)S(1)} collective-permute-done((f32[1024,128]{1,0:T(8,128)S(1)}, f32[1024,128]{1,0:T(8,128)S(1)}, u32[]{:S(2)}, u32[]{:S(2)}) %collective-permute-start.20) | collective-permute-done | bytes 524320 | tf_op jit(solution)/shard_map/ppermute | solution.py:76
  39.5 6.0 %collective-permute-done.2 = f32[1024,128]{1,0:T(8,128)S(1)} collective-permute-done((f32[1024,128]{1,0:T(8,128)S(1)}, f32[1024,128]{1,0:T(8,128)S(1)}, u32[]{:S(2)}, u32[]{:S(2)}) %collective-permute-start.2) | collective-permute-done | bytes 524320 | tf_op jit(solution)/shard_map/ppermute | solution.py:76
  59.7 7.9 %collective-permute-done.25 = f32[256,128]{1,0:T(8,128)S(1)} collective-permute-done((f32[256,128]{1,0:T(8,128)S(1)}, f32[256,128]{1,0:T(8,128)S(1)}, u32[]{:S(2)}, u32[]{:S(2)}) %collective-permute-start.25) | collective-permute-done | bytes 131104 | tf_op jit(solution)/shard_map/ppermute | solution.py:76
  87.8 11.7 %collective-permute-done.9.refs_1_.refs_5_ = f32[1024,128]{1,0:T(8,128)S(1)} collective-permute-done((f32[1024,128]{1,0:T(8,128)S(1)}, f32[1024,128]{1,0:T(8,128)S(1)}, u32[]{:S(2)}, u32[]{:S(2)}) %collective-permute-start.9) | collective-permute-done | bytes 524320 | tf_op jit(solution)/shard_map/ppermute | solution.py:76
  99.6 7.1 %features.4 = (f32[256,128]{1,0:T(8,128)}, f32[256,128]{1,0:T(8,128)}) custom-call(s32[17]{0:T(128)} %stack.77.meta_ref, s32[2]{0:T(128)} %offsets_ref.5, s32[16384]{0:T(1024)} %ids_ref.5, f32[64,16384]{1,0:T(8,128)} %bitcast.23, f32[128,128]{1,0:T(8,128)} %bitcast.35, f32[64,1024]{1,0:T(8,128)} %bitcast.26), custom_call_target="tpu_custom_call" | custom-call | tf_op jit(solution)/shard_map/features/pallas_call | solution.py:268
  107.8 7.8 %shard_map.77 = (f32[1024,128]{1,0:T(8,128)}, f32[1024,128]{1,0:T(8,128)}, f32[1024,128]{1,0:T(8,128)}, f32[1024,128]{1,0:T(8,128)}) custom-call(s32[17]{0:T(128)} %stack.77.meta_ref, f32[4,4096,256]{2,1,0:T(8,128)} %diag_ref.15, f32[6,256,4096]{2,1,0:T(8,128)} %lower_ref.19, f32[256,128]{1,0:T(8,128)} %get-tuple-element.77.pending_ref, ...), custom_call_target="tpu_custom_call" | custom-call | tf_op jit(solution)/shard_map/pallas_call | solution.py:210
  116.1 8.0 %shard_map.74 = (f32[1024,128]{1,0:T(8,128)}, f32[1024,128]{1,0:T(8,128)}, f32[1024,128]{1,0:T(8,128)}, f32[1024,128]{1,0:T(8,128)}) custom-call(s32[17]{0:T(128)} %stack.77.meta_ref, f32[4,4096,256]{2,1,0:T(8,128)} %diag_ref.15, f32[6,256,4096]{2,1,0:T(8,128)} %lower_ref.19, f32[256,128]{1,0:T(8,128)} %get-tuple-element.56.pending_ref, ...), custom_call_target="tpu_custom_call" | custom-call | tf_op jit(solution)/shard_map/pallas_call | solution.py:210
  128.9 10.6 %collective-permute-done.44 = f32[1024,128]{1,0:T(8,128)S(1)} collective-permute-done((f32[1024,128]{1,0:T(8,128)S(1)}, f32[1024,128]{1,0:T(8,128)S(1)}, u32[]{:S(2)}, u32[]{:S(2)}) %collective-permute-start.44) | collective-permute-done | bytes 524320 | tf_op jit(solution)/shard_map/ppermute | solution.py:76
  144.1 5.9 %collective-permute-done.14 = f32[1024,128]{1,0:T(8,128)S(1)} collective-permute-done((f32[1024,128]{1,0:T(8,128)S(1)}, f32[1024,128]{1,0:T(8,128)S(1)}, u32[]{:S(2)}, u32[]{:S(2)}) %collective-permute-start.14) | collective-permute-done | bytes 524320 | tf_op jit(solution)/shard_map/ppermute | solution.py:76
  160.5 8.3 %collective-permute-done.49 = f32[256,128]{1,0:T(8,128)S(1)} collective-permute-done((f32[256,128]{1,0:T(8,128)S(1)}, f32[256,128]{1,0:T(8,128)S(1)}, u32[]{:S(2)}, u32[]{:S(2)}) %collective-permute-start.49) | collective-permute-done | bytes 131104 | tf_op jit(solution)/shard_map/ppermute | solution.py:76
  190.7 11.7 %collective-permute-done.33.refs_1_.refs_3_ = f32[1024,128]{1,0:T(8,128)S(1)} collective-permute-done((f32[1024,128]{1,0:T(8,128)S(1)}, f32[1024,128]{1,0:T(8,128)S(1)}, u32[]{:S(2)}, u32[]{:S(2)}) %collective-permute-start.33) | collective-permute-done | bytes 524320 | tf_op jit(solution)/shard_map/ppermute | solution.py:76
  202.4 11.2 %features.5 = (f32[256,128]{1,0:T(8,128)}, f32[256,128]{1,0:T(8,128)}, f32[256,128]{1,0:T(8,128)}, f32[256,128]{1,0:T(8,128)}) custom-call(s32[17]{0:T(128)} %stack.77.meta_ref, s32[2]{0:T(128)} %offsets_ref.5, s32[16384]{0:T(1024)} %ids_ref.5, f32[64,16384]{1,0:T(8,128)} %bitcast.24, f32[128,128]{1,0:T(8,128)} %bitcast.36, f32[64,1024]{1,0:T(8,128)} %bitcast.27), custom_call_target="tpu_custom_call" | custom-call | tf_op jit(solution)/shard_map/features/pallas_call | solution.py:268
  213.6 9.7 %older.2 = (f32[256,128]{1,0:T(8,128)}, f32[256,128]{1,0:T(8,128)}, f32[256,128]{1,0:T(8,128)}, f32[256,128]{1,0:T(8,128)}) custom-call(s32[17]{0:T(128)} %stack.77.meta_ref, f32[6,256,4096]{2,1,0:T(8,128)} %lower_ref.19, f32[256,128]{1,0:T(8,128)} %get-tuple-element.61.refs_0_, f32[256,128]{1,0:T(8,128)} %get-tuple-element.62.refs_1_, ...), custom_call_target="tpu_custom_call" | custom-call | tf_op jit(solution)/shard_map/older/pallas_call | solution.py:307
  224.4 7.8 %shard_map.79 = (f32[1024,128]{1,0:T(8,128)}, f32[1024,128]{1,0:T(8,128)}, f32[1024,128]{1,0:T(8,128)}, f32[1024,128]{1,0:T(8,128)}) custom-call(s32[17]{0:T(128)} %stack.77.meta_ref, f32[4,4096,256]{2,1,0:T(8,128)} %diag_ref.15, f32[6,256,4096]{2,1,0:T(8,128)} %lower_ref.19, f32[256,128]{1,0:T(8,128)} %get-tuple-element.87.pending_ref, ...), custom_call_target="tpu_custom_call" | custom-call | tf_op jit(solution)/shard_map/pallas_call | solution.py:210
  232.6 8.0 %shard_map.76 = (f32[1024,128]{1,0:T(8,128)}, f32[1024,128]{1,0:T(8,128)}, f32[1024,128]{1,0:T(8,128)}, f32[1024,128]{1,0:T(8,128)}) custom-call(s32[17]{0:T(128)} %stack.77.meta_ref, f32[4,4096,256]{2,1,0:T(8,128)} %diag_ref.15, f32[6,256,4096]{2,1,0:T(8,128)} %lower_ref.19, f32[256,128]{1,0:T(8,128)} %get-tuple-element.70.pending_ref, ...), custom_call_target="tpu_custom_call" | custom-call | tf_op jit(solution)/shard_map/pallas_call | solution.py:210
  245.4 10.6 %collective-permute-done.68 = f32[1024,128]{1,0:T(8,128)S(1)} collective-permute-done((f32[1024,128]{1,0:T(8,128)S(1)}, f32[1024,128]{1,0:T(8,128)S(1)}, u32[]{:S(2)}, u32[]{:S(2)}) %collective-permute-start.68) | collective-permute-done | bytes 524320 | tf_op jit(solution)/shard_map/ppermute | solution.py:76
  260.7 5.9 %collective-permute-done.38 = f32[1024,128]{1,0:T(8,128)S(1)} collective-permute-done((f32[1024,128]{1,0:T(8,128)S(1)}, f32[1024,128]{1,0:T(8,128)S(1)}, u32[]{:S(2)}, u32[]{:S(2)}) %collective-permute-start.38) | collective-permute-done | bytes 524320 | tf_op jit(solution)/shard_map/ppermute | solution.py:76
  277.4 7.5 %collective-permute-done.73 = f32[256,128]{1,0:T(8,128)S(1)} collective-permute-done((f32[256,128]{1,0:T(8,128)S(1)}, f32[256,128]{1,0:T(8,128)S(1)}, u32[]{:S(2)}, u32[]{:S(2)}) %collective-permute-start.73) | collective-permute-done | bytes 131104 | tf_op jit(solution)/shard_map/ppermute | solution.py:76
  307.2 11.7 %collective-permute-done.57.refs_1_ = f32[1024,128]{1,0:T(8,128)S(1)} collective-permute-done((f32[1024,128]{1,0:T(8,128)S(1)}, f32[1024,128]{1,0:T(8,128)S(1)}, u32[]{:S(2)}, u32[]{:S(2)}) %collective-permute-start.57) | collective-permute-done | bytes 524320 | tf_op jit(solution)/shard_map/ppermute | solution.py:76
  318.9 7.1 %older.3 = (f32[256,128]{1,0:T(8,128)}, f32[256,128]{1,0:T(8,128)}) custom-call(s32[17]{0:T(128)} %stack.77.meta_ref, f32[6,256,4096]{2,1,0:T(8,128)} %lower_ref.19, f32[256,128]{1,0:T(8,128)} %get-tuple-element.75.refs_0_, f32[256,128]{1,0:T(8,128)} %get-tuple-element.76.refs_1_, f32[1024,128]{1,0:T(8,128)} %copy-done.2, f32[1024,128]{1,0:T(8,128)} %copy-done.6, ...), custom_call_target="tpu_custom_call" | custom-call | tf_op jit(solution)/shard_map/older/pallas_call | solution.py:307
  326.1 7.8 %shard_map.80 = (f32[1024,128]{1,0:T(8,128)}, f32[1024,128]{1,0:T(8,128)}, f32[1024,128]{1,0:T(8,128)}, f32[1024,128]{1,0:T(8,128)}) custom-call(s32[17]{0:T(128)} %stack.77.meta_ref, f32[4,4096,256]{2,1,0:T(8,128)} %diag_ref.15, f32[6,256,4096]{2,1,0:T(8,128)} %lower_ref.19, f32[256,128]{1,0:T(8,128)} %get-tuple-element.92.pending_ref, ...), custom_call_target="tpu_custom_call" | custom-call | tf_op jit(solution)/shard_map/pallas_call | solution.py:210
  335.1 8.0 %shard_map.78 = (f32[1024,128]{1,0:T(8,128)}, f32[1024,128]{1,0:T(8,128)}, f32[1024,128]{1,0:T(8,128)}, f32[1024,128]{1,0:T(8,128)}) custom-call(s32[17]{0:T(128)} %stack.77.meta_ref, f32[4,4096,256]{2,1,0:T(8,128)} %diag_ref.15, f32[6,256,4096]{2,1,0:T(8,128)} %lower_ref.19, f32[256,128]{1,0:T(8,128)} %get-tuple-element.82.pending_ref, ...), custom_call_target="tpu_custom_call" | custom-call | tf_op jit(solution)/shard_map/pallas_call | solution.py:210
  347.9 10.6 %collective-permute-done.80 = f32[1024,128]{1,0:T(8,128)S(1)} collective-permute-done((f32[1024,128]{1,0:T(8,128)S(1)}, f32[1024,128]{1,0:T(8,128)S(1)}, u32[]{:S(2)}, u32[]{:S(2)}) %collective-permute-start.80) | collective-permute-done | bytes 524320 | tf_op jit(solution)/shard_map/ppermute | solution.py:76
  (251 shorter events, 175.5 us)
Async XLA Ops:
  21.8 17.7 %collective-permute-start = (f32[1024,128]{1,0:T(8,128)}, f32[1024,128]{1,0:T(8,128)S(1)}, u32[]{:S(2)}, u32[]{:S(2)}) collective-permute-start(f32[1024,128]{1,0:T(8,128)} %get-tuple-element.53), channel_id=1, source_target_pairs={{0,1},{1,0},{2,3},{3,2},{4,5},{5,4},{6,7},{7,6},{8,9},{9,8},{10,11... | collective-permute-start | bytes 1572872 | tf_op jit(solution)/shard_map/ppermute | solution.py:76
  23.1 22.5 %collective-permute-start.2 = (f32[1024,128]{1,0:T(8,128)S(1)}, f32[1024,128]{1,0:T(8,128)S(1)}, u32[]{:S(2)}, u32[]{:S(2)}) collective-permute-start(f32[1024,128]{1,0:T(8,128)S(1)} %add.176), channel_id=1, source_target_pairs={{0,2},{1,3},{2,0},{3,1},{4,6},{5,7},{6,4},{7,5},{8,10},{9,11},{10,... | collective-permute-start | bytes 1572872 | tf_op jit(solution)/shard_map/ppermute | solution.py:76
  56.2 16.9 %collective-permute-start.4 = (f32[256,128]{1,0:T(8,128)S(1)}, f32[256,128]{1,0:T(8,128)S(1)}, u32[]{:S(2)}, u32[]{:S(2)}) collective-permute-start(f32[256,128]{1,0:T(8,128)S(1)} %get-tuple-element.120), channel_id=1, source_target_pairs={{0,8},{1,9},{2,10},{3,11},{4,12},{5,13},{6,14},{7,15},{8,0},{9,1},... | collective-permute-start | bytes 393224 | tf_op jit(solution)/shard_map/ppermute | solution.py:76
  67.6 19.6 %collective-permute-start.27 = (f32[1024,128]{1,0:T(8,128)S(1)}, f32[1024,128]{1,0:T(8,128)S(1)}, u32[]{:S(2)}, u32[]{:S(2)}) collective-permute-start(f32[1024,128]{1,0:T(8,128)S(1)} %pad_maximum_fusion.1.refs_8_.refs_0_), channel_id=1, source_target_pairs={{0,2},{1,3},{2,0},{3,1},{4,6},{5,7},{6,4},{7,5},{8,10},{9,11},{10,... | collective-permute-start | bytes 1572872 | tf_op jit(solution)/shard_map/ppermute | solution.py:76
  87.2 19.5 %collective-permute-start.28 = (f32[1024,128]{1,0:T(8,128)S(1)}, f32[1024,128]{1,0:T(8,128)S(1)}, u32[]{:S(2)}, u32[]{:S(2)}) collective-permute-start(f32[1024,128]{1,0:T(8,128)S(1)} %pad_maximum_fusion.1.refs_8_.refs_0_), channel_id=1, source_target_pairs={{0,1},{1,0},{2,3},{3,2},{4,5},{5,4},{6,7},{7,6},{8,9},{9,8},{10,11... | collective-permute-start | bytes 1572872 | tf_op jit(solution)/shard_map/ppermute | solution.py:76
  87.3 19.5 %collective-permute-start.29 = (f32[1024,128]{1,0:T(8,128)S(1)}, f32[1024,128]{1,0:T(8,128)S(1)}, u32[]{:S(2)}, u32[]{:S(2)}) collective-permute-start(f32[1024,128]{1,0:T(8,128)S(1)} %collective-permute-done.27.refs_9_.refs_1_), channel_id=1, source_target_pairs={{0,1},{1,0},{2,3},{3,2},{4,5},{5,4},{6,7},{7,6},{8,9},{9,8},{10,11... | collective-permute-start | bytes 1572872 | tf_op jit(solution)/shard_map/ppermute | solution.py:76
  87.8 28.3 %collective-permute-start.10 = (f32[1024,128]{1,0:T(8,128)S(1)}, f32[1024,128]{1,0:T(8,128)}, u32[]{:S(2)}, u32[]{:S(2)}) collective-permute-start(f32[1024,128]{1,0:T(8,128)S(1)} %pad_maximum_fusion.refs_0_.refs_4_), channel_id=1, source_target_pairs={{0,1},{1,0},{2,3},{3,2},{4,5},{5,4},{6,7},{7,6},{8,9},{9,8},{10,11... | collective-permute-start | bytes 1572872 | tf_op jit(solution)/shard_map/ppermute | solution.py:76
  126.3 17.9 %collective-permute-start.12 = (f32[1024,128]{1,0:T(8,128)}, f32[1024,128]{1,0:T(8,128)S(1)}, u32[]{:S(2)}, u32[]{:S(2)}) collective-permute-start(f32[1024,128]{1,0:T(8,128)} %get-tuple-element.58), channel_id=1, source_target_pairs={{0,1},{1,0},{2,3},{3,2},{4,5},{5,4},{6,7},{7,6},{8,9},{9,8},{10,11... | collective-permute-start | bytes 1572872 | tf_op jit(solution)/shard_map/ppermute | solution.py:76
  127.4 22.6 %collective-permute-start.14 = (f32[1024,128]{1,0:T(8,128)S(1)}, f32[1024,128]{1,0:T(8,128)S(1)}, u32[]{:S(2)}, u32[]{:S(2)}) collective-permute-start(f32[1024,128]{1,0:T(8,128)S(1)} %add.182), channel_id=1, source_target_pairs={{0,2},{1,3},{2,0},{3,1},{4,6},{5,7},{6,4},{7,5},{8,10},{9,11},{10,... | collective-permute-start | bytes 1572872 | tf_op jit(solution)/shard_map/ppermute | solution.py:76
  158.1 17.4 %collective-permute-start.16 = (f32[256,128]{1,0:T(8,128)S(1)}, f32[256,128]{1,0:T(8,128)S(1)}, u32[]{:S(2)}, u32[]{:S(2)}) collective-permute-start(f32[256,128]{1,0:T(8,128)S(1)} %get-tuple-element.114), channel_id=1, source_target_pairs={{0,8},{1,9},{2,10},{3,11},{4,12},{5,13},{6,14},{7,15},{8,0},{9,1},... | collective-permute-start | bytes 393224 | tf_op jit(solution)/shard_map/ppermute | solution.py:76
  168.9 21.2 %collective-permute-start.51 = (f32[1024,128]{1,0:T(8,128)S(1)}, f32[1024,128]{1,0:T(8,128)S(1)}, u32[]{:S(2)}, u32[]{:S(2)}) collective-permute-start(f32[1024,128]{1,0:T(8,128)S(1)} %pad_maximum_fusion.3.refs_6_.refs_0_), channel_id=1, source_target_pairs={{0,2},{1,3},{2,0},{3,1},{4,6},{5,7},{6,4},{7,5},{8,10},{9,11},{10,... | collective-permute-start | bytes 1572872 | tf_op jit(solution)/shard_map/ppermute | solution.py:76
  190.1 33.3 %collective-permute-start.52 = (f32[1024,128]{1,0:T(8,128)S(1)}, f32[1024,128]{1,0:T(8,128)S(1)}, u32[]{:S(2)}, u32[]{:S(2)}) collective-permute-start(f32[1024,128]{1,0:T(8,128)S(1)} %pad_maximum_fusion.3.refs_6_.refs_0_), channel_id=1, source_target_pairs={{0,1},{1,0},{2,3},{3,2},{4,5},{5,4},{6,7},{7,6},{8,9},{9,8},{10,11... | collective-permute-start | bytes 1572872 | tf_op jit(solution)/shard_map/ppermute | solution.py:76
  190.1 33.3 %collective-permute-start.53 = (f32[1024,128]{1,0:T(8,128)S(1)}, f32[1024,128]{1,0:T(8,128)S(1)}, u32[]{:S(2)}, u32[]{:S(2)}) collective-permute-start(f32[1024,128]{1,0:T(8,128)S(1)} %collective-permute-done.51.refs_7_.refs_1_), channel_id=1, source_target_pairs={{0,1},{1,0},{2,3},{3,2},{4,5},{5,4},{6,7},{7,6},{8,9},{9,8},{10,11... | collective-permute-start | bytes 1572872 | tf_op jit(solution)/shard_map/ppermute | solution.py:76
  190.6 42.0 %collective-permute-start.34 = (f32[1024,128]{1,0:T(8,128)S(1)}, f32[1024,128]{1,0:T(8,128)}, u32[]{:S(2)}, u32[]{:S(2)}) collective-permute-start(f32[1024,128]{1,0:T(8,128)S(1)} %pad_maximum_fusion.2.refs_0_.refs_2_), channel_id=1, source_target_pairs={{0,1},{1,0},{2,3},{3,2},{4,5},{5,4},{6,7},{7,6},{8,9},{9,8},{10,11... | collective-permute-start | bytes 1572872 | tf_op jit(solution)/shard_map/ppermute | solution.py:76
  202.4 30.2 %collective-permute-start.35 = (f32[1024,128]{1,0:T(8,128)S(1)}, f32[1024,128]{1,0:T(8,128)}, u32[]{:S(2)}, u32[]{:S(2)}) collective-permute-start(f32[1024,128]{1,0:T(8,128)S(1)} %collective-permute-done.33.refs_1_.refs_3_), channel_id=1, source_target_pairs={{0,1},{1,0},{2,3},{3,2},{4,5},{5,4},{6,7},{7,6},{8,9},{9,8},{10,11... | collective-permute-start | bytes 1572872 | tf_op jit(solution)/shard_map/ppermute | solution.py:76
  242.8 17.9 %collective-permute-start.36 = (f32[1024,128]{1,0:T(8,128)}, f32[1024,128]{1,0:T(8,128)S(1)}, u32[]{:S(2)}, u32[]{:S(2)}) collective-permute-start(f32[1024,128]{1,0:T(8,128)} %get-tuple-element.72), channel_id=1, source_target_pairs={{0,1},{1,0},{2,3},{3,2},{4,5},{5,4},{6,7},{7,6},{8,9},{9,8},{10,11... | collective-permute-start | bytes 1572872 | tf_op jit(solution)/shard_map/ppermute | solution.py:76
  243.9 22.6 %collective-permute-start.38 = (f32[1024,128]{1,0:T(8,128)S(1)}, f32[1024,128]{1,0:T(8,128)S(1)}, u32[]{:S(2)}, u32[]{:S(2)}) collective-permute-start(f32[1024,128]{1,0:T(8,128)S(1)} %add.194), channel_id=1, source_target_pairs={{0,2},{1,3},{2,0},{3,1},{4,6},{5,7},{6,4},{7,5},{8,10},{9,11},{10,... | collective-permute-start | bytes 1572872 | tf_op jit(solution)/shard_map/ppermute | solution.py:76
  274.9 17.1 %collective-permute-start.40 = (f32[256,128]{1,0:T(8,128)S(1)}, f32[256,128]{1,0:T(8,128)S(1)}, u32[]{:S(2)}, u32[]{:S(2)}) collective-permute-start(f32[256,128]{1,0:T(8,128)S(1)} %get-tuple-element.102), channel_id=1, source_target_pairs={{0,8},{1,9},{2,10},{3,11},{4,12},{5,13},{6,14},{7,15},{8,0},{9,1},... | collective-permute-start | bytes 393224 | tf_op jit(solution)/shard_map/ppermute | solution.py:76
  285.0 21.6 %collective-permute-start.75 = (f32[1024,128]{1,0:T(8,128)S(1)}, f32[1024,128]{1,0:T(8,128)S(1)}, u32[]{:S(2)}, u32[]{:S(2)}) collective-permute-start(f32[1024,128]{1,0:T(8,128)S(1)} %pad_maximum_fusion.5.refs_0_), channel_id=1, source_target_pairs={{0,2},{1,3},{2,0},{3,1},{4,6},{5,7},{6,4},{7,5},{8,10},{9,11},{10,... | collective-permute-start | bytes 1572872 | tf_op jit(solution)/shard_map/ppermute | solution.py:76
  306.6 19.4 %collective-permute-start.76 = (f32[1024,128]{1,0:T(8,128)S(1)}, f32[1024,128]{1,0:T(8,128)}, u32[]{:S(2)}, u32[]{:S(2)}) collective-permute-start(f32[1024,128]{1,0:T(8,128)S(1)} %pad_maximum_fusion.5.refs_0_), channel_id=1, source_target_pairs={{0,1},{1,0},{2,3},{3,2},{4,5},{5,4},{6,7},{7,6},{8,9},{9,8},{10,11... | collective-permute-start | bytes 1572872 | tf_op jit(solution)/shard_map/ppermute | solution.py:76
  306.6 19.4 %collective-permute-start.77 = (f32[1024,128]{1,0:T(8,128)S(1)}, f32[1024,128]{1,0:T(8,128)}, u32[]{:S(2)}, u32[]{:S(2)}) collective-permute-start(f32[1024,128]{1,0:T(8,128)S(1)} %collective-permute-done.75.refs_1_), channel_id=1, source_target_pairs={{0,1},{1,0},{2,3},{3,2},{4,5},{5,4},{6,7},{7,6},{8,9},{9,8},{10,11... | collective-permute-start | bytes 1572872 | tf_op jit(solution)/shard_map/ppermute | solution.py:76
  307.1 27.2 %collective-permute-start.58 = (f32[1024,128]{1,0:T(8,128)S(1)}, f32[1024,128]{1,0:T(8,128)S(1)}, u32[]{:S(2)}, u32[]{:S(2)}) collective-permute-start(f32[1024,128]{1,0:T(8,128)S(1)} %pad_maximum_fusion.4.refs_0_), channel_id=1, source_target_pairs={{0,1},{1,0},{2,3},{3,2},{4,5},{5,4},{6,7},{7,6},{8,9},{9,8},{10,11... | collective-permute-start | bytes 1572872 | tf_op jit(solution)/shard_map/ppermute | solution.py:76
  345.3 18.9 %collective-permute-start.60 = (f32[1024,128]{1,0:T(8,128)}, f32[1024,128]{1,0:T(8,128)S(1)}, u32[]{:S(2)}, u32[]{:S(2)}) collective-permute-start(f32[1024,128]{1,0:T(8,128)} %get-tuple-element.84), channel_id=1, source_target_pairs={{0,1},{1,0},{2,3},{3,2},{4,5},{5,4},{6,7},{7,6},{8,9},{9,8},{10,11... | collective-permute-start | bytes 1572872 | tf_op jit(solution)/shard_map/ppermute | solution.py:76
  346.4 22.6 %collective-permute-start.62 = (f32[1024,128]{1,0:T(8,128)S(1)}, f32[1024,128]{1,0:T(8,128)S(1)}, u32[]{:S(2)}, u32[]{:S(2)}) collective-permute-start(f32[1024,128]{1,0:T(8,128)S(1)} %add.206), channel_id=1, source_target_pairs={{0,2},{1,3},{2,0},{3,1},{4,6},{5,7},{6,4},{7,5},{8,10},{9,11},{10,... | collective-permute-start | bytes 1572872 | tf_op jit(solution)/shard_map/ppermute | solution.py:76
  (87 other events, 1181.0 us)
